TPU v7x, 32 devices: a whole 2x2x4 slice. The times are simulated.
32 devices in a mesh: nodes: 32 (over z, y, x, core).
Axes of the slice: x: 2, y: 2, z: 4, core: 2. Of those that a mesh axis runs over, the one named last changes fastest.
Arguments:
- rhs: bfloat16 [4, 20480, 256], P(None, 'nodes'), may hold values from -6 to 6
- inv_diag: bfloat16 [4, 20480, 640], P(None, 'nodes'), as said below
- factor: bfloat16 [3, 49152, 640], P(None, 'nodes'), may hold values from -0.15625 to 0.15625
- tile_list: int32 [3, 32, 12], P(None, 'nodes'), may hold values from 0 to 239, as said below
- live_count: int32 [3, 32], P(None, 'nodes'), may hold values from 4 to 12, as said below
Outputs:
- solution: float32 [4, 20480, 256], P(None, 'nodes')
Inputs may be any that keep to these rules, and one draw needn't show every extreme that they name: `tile_list`: entries at first index i name tiles of levels 0 to i only: they are below (i + 1) * 2 * 8 * 5. `live_count`: in every level some supernode has all 12 slots in use. `inv_diag`: each 640 by 640 block is upper triangular: zero below its diagonal, diagonal entries between 0.5 and 2.
All inputs are finite; a program needn't handle non-finite values.
Results may differ from a plain program's by a relative error of at most 0.004.
Values may be sent and summed in bfloat16 or wider, within the bound.
No kernel may reach another device: no remote copies, remote signals or barrier semaphores. Data moves between devices by JAX's collectives and lax.ppermute only.
A program may use at most 128 MiB of HBM per device.

v0:
```python
import jax
import jax.numpy as jnp
from jax import lax
from jax.sharding import PartitionSpec as P

TILE = 128
SLOTS = 12
GROUP = 8


def swapped(shard, axis, stride):
    return lax.ppermute(shard, axis, [(i, i ^ 1 << stride) for i in range(lax.axis_size(axis))])


def shifted(block, axis, distance):
    devices = range(lax.axis_size(axis))
    route = [((i - distance) % len(devices), i) for i in devices]
    return lax.ppermute(block, axis, route)


def gather_group(pieces):
    gathered = pieces[None]
    position = lax.axis_index("nodes")
    for bit_index in range(GROUP.bit_length() - 1):
        partner = swapped(gathered, "nodes", bit_index)
        upper_half = position >> bit_index & 1 == 1
        gathered = jnp.where(
            upper_half,
            jnp.concatenate([partner, gathered], 0),
            jnp.concatenate([gathered, partner], 0),
        )
    return gathered


def spread(solved):
    own_group = gather_group(solved[None])[:, 0]
    previous = shifted(own_group, "nodes", GROUP)
    return jnp.concatenate([previous, own_group], 0)


def subtract(pool, factor_rows, indices, count):
    columns = pool.shape[2]
    picked = jnp.take(pool, indices, axis=0)
    live_mask = jnp.arange(SLOTS) < count
    picked = jnp.where(live_mask[:, None, None], picked, jnp.zeros_like(picked))
    return lax.dot_general(
        factor_rows,
        picked.reshape(SLOTS * TILE, columns),
        (((0,), (0,)), ((), ())),
        preferred_element_type=jnp.float32,
    )


def solve_columns(right, inv_diag, factor, tile_list, live_count):
    pooled = []
    solved_all = []
    height_count = right.shape[0]
    for height_index in range(height_count):
        updated = right[height_index].astype(jnp.float32)
        if height_index > 0:
            pool = jnp.concatenate(pooled, 0)
            updated = updated - subtract(
                pool,
                factor[height_index - 1],
                tile_list[height_index - 1, 0],
                live_count[height_index - 1, 0],
            )
        rounded = updated.astype(jnp.bfloat16)
        solution = jnp.dot(inv_diag[height_index], rounded, preferred_element_type=jnp.float32)
        solved_all.append(solution)
        if height_index < height_count - 1:
            spread_out = spread(solution.astype(jnp.bfloat16))
            pooled.append(spread_out.reshape(-1, TILE, spread_out.shape[2]))
    return jnp.stack(solved_all)


def body(rhs, inv_diag, factor, tile_list, live_count):
    width_k = rhs.shape[2]
    bounds = [(0, width_k // 2), (width_k // 2, width_k)]
    results = []
    for first_col, last_col in bounds:
        results.append(
            solve_columns(rhs[:, :, first_col:last_col], inv_diag, factor, tile_list, live_count)
        )
    return jnp.concatenate(results, 2)


def solution(mesh):
    return jax.shard_map(
        body,
        mesh=mesh,
        in_specs=(
            P(None, "nodes", None),
            P(None, "nodes", None),
            P(None, "nodes", None),
            P(None, "nodes", None),
            P(None, "nodes"),
        ),
        out_specs=P(None, "nodes", None),
        check_vma=False,
    )
```

profile of v0, /device:TPU:0, one launch (start us, length us, event | category | flops | bytes accessed | tf_op | source)
XLA Modules:
  0.0 312.4 jit_solution(14821495101247354807)
XLA Ops:
  8.1 7.5 %collective-permute-done.13 = bf16[2,1,640,128]{3,2,0,1:T(8,128)(2,1)S(1)} collective-permute-done((bf16[2,1,640,128]{3,2,0,1:T(8,128)(2,1)S(1)}, bf16[2,1,640,128]{3,2,0,1:T(8,128)(2,1)S(1)}, u32[]{:S(2)}, u32[]{:S(2)}) %collective-permute-start.13) | collective-permute-done | bytes 327712 | tf_op jit(solution)/shard_map/ppermute | solution.py:12
  17.8 4.1 %collective-permute-done.1 = bf16[2,1,640,128]{3,2,0,1:T(8,128)(2,1)S(1)} collective-permute-done((bf16[2,1,640,128]{3,2,0,1:T(8,128)(2,1)S(1)}, bf16[2,1,640,128]{3,2,0,1:T(8,128)(2,1)S(1)}, u32[]{:S(2)}, u32[]{:S(2)}) %collective-permute-start.1) | collective-permute-done | bytes 327712 | tf_op jit(solution)/shard_map/ppermute | solution.py:12
  24.0 9.5 %collective-permute-done.14 = bf16[4,1,640,128]{3,2,0,1:T(8,128)(2,1)} collective-permute-done((bf16[4,1,640,128]{3,2,0,1:T(8,128)(2,1)S(1)}, bf16[4,1,640,128]{3,2,0,1:T(8,128)(2,1)}, u32[]{:S(2)}, u32[]{:S(2)}) %collective-permute-start.14) | collective-permute-done | bytes 655392 | tf_op jit(solution)/shard_map/ppermute | solution.py:12
  37.2 8.1 %collective-permute-done.2 = bf16[4,1,640,128]{3,2,0,1:T(8,128)(2,1)} collective-permute-done((bf16[4,1,640,128]{3,2,0,1:T(8,128)(2,1)S(1)}, bf16[4,1,640,128]{3,2,0,1:T(8,128)(2,1)}, u32[]{:S(2)}, u32[]{:S(2)}) %collective-permute-start.2) | collective-permute-done | bytes 655392 | tf_op jit(solution)/shard_map/ppermute | solution.py:12
  50.8 18.0 %collective-permute-done.15 = bf16[8,640,128]{2,1,0:T(8,128)(2,1)S(1)} collective-permute-done((bf16[8,640,128]{2,1,0:T(8,128)(2,1)S(1)}, bf16[8,640,128]{2,1,0:T(8,128)(2,1)S(1)}, u32[]{:S(2)}, u32[]{:S(2)}) %collective-permute-start.15) | collective-permute-done | bytes 1310752 | tf_op jit(solution)/shard_map/ppermute | solution.py:18
  70.5 20.9 %collective-permute-done.3 = bf16[8,640,128]{2,1,0:T(8,128)(2,1)} collective-permute-done((bf16[8,640,128]{2,1,0:T(8,128)(2,1)}, bf16[8,640,128]{2,1,0:T(8,128)(2,1)}, u32[]{:S(2)}, u32[]{:S(2)}) %collective-permute-start.3) | collective-permute-done | bytes 1310752 | tf_op jit(solution)/shard_map/ppermute | solution.py:18
  99.1 4.0 %fusion.73 = f32[128,640]{0,1:T(8,128)} fusion(bf16[1536,128]{1,0:T(8,128)(2,1)} %bitcast.379, bf16[3,1536,640]{2,1,0:T(8,128)(2,1)} %param.13, bf16[4,640,640]{2,1,0:T(8,128)(2,1)} %param.12, bf16[4,640,256]{2,1,0:T(8,128)(2,1)} %param.11), kind=kOutput, calls=%fused_computation.61 | convolution fusion | flops 356761600 | bytes 3670016 | tf_op jit(solution)/shard_map/dot_general | solution.py:69
  108.0 8.4 %collective-permute-done.17 = bf16[2,1,640,128]{3,2,0,1:T(8,128)(2,1)S(1)} collective-permute-done((bf16[2,1,640,128]{3,2,0,1:T(8,128)(2,1)S(1)}, bf16[2,1,640,128]{3,2,0,1:T(8,128)(2,1)S(1)}, u32[]{:S(2)}, u32[]{:S(2)}) %collective-permute-start.17) | collective-permute-done | bytes 327712 | tf_op jit(solution)/shard_map/ppermute | solution.py:12
  117.6 4.8 %collective-permute-done.5 = bf16[2,1,640,128]{3,2,0,1:T(8,128)(2,1)S(1)} collective-permute-done((bf16[2,1,640,128]{3,2,0,1:T(8,128)(2,1)S(1)}, bf16[2,1,640,128]{3,2,0,1:T(8,128)(2,1)S(1)}, u32[]{:S(2)}, u32[]{:S(2)}) %collective-permute-start.5) | collective-permute-done | bytes 327712 | tf_op jit(solution)/shard_map/ppermute | solution.py:12
  123.8 10.3 %collective-permute-done.18 = bf16[4,1,640,128]{3,2,0,1:T(8,128)(2,1)S(1)} collective-permute-done((bf16[4,1,640,128]{3,2,0,1:T(8,128)(2,1)S(1)}, bf16[4,1,640,128]{3,2,0,1:T(8,128)(2,1)S(1)}, u32[]{:S(2)}, u32[]{:S(2)}) %collective-permute-start.18) | collective-permute-done | bytes 655392 | tf_op jit(solution)/shard_map/ppermute | solution.py:12
  134.6 10.9 %collective-permute-done.6 = bf16[4,1,640,128]{3,2,0,1:T(8,128)(2,1)S(1)} collective-permute-done((bf16[4,1,640,128]{3,2,0,1:T(8,128)(2,1)S(1)}, bf16[4,1,640,128]{3,2,0,1:T(8,128)(2,1)S(1)}, u32[]{:S(2)}, u32[]{:S(2)}) %collective-permute-start.6) | collective-permute-done | bytes 655392 | tf_op jit(solution)/shard_map/ppermute | solution.py:12
  146.6 21.3 %collective-permute-done.19 = bf16[8,640,128]{2,1,0:T(8,128)(2,1)S(1)} collective-permute-done((bf16[8,640,128]{2,1,0:T(8,128)(2,1)S(1)}, bf16[8,640,128]{2,1,0:T(8,128)(2,1)S(1)}, u32[]{:S(2)}, u32[]{:S(2)}) %collective-permute-start.19) | collective-permute-done | bytes 1310752 | tf_op jit(solution)/shard_map/ppermute | solution.py:18
  171.2 18.4 %collective-permute-done.7 = bf16[8,640,128]{2,1,0:T(8,128)(2,1)S(1)} collective-permute-done((bf16[8,640,128]{2,1,0:T(8,128)(2,1)S(1)}, bf16[8,640,128]{2,1,0:T(8,128)(2,1)S(1)}, u32[]{:S(2)}, u32[]{:S(2)}) %collective-permute-start.7) | collective-permute-done | bytes 1310752 | tf_op jit(solution)/shard_map/ppermute | solution.py:18
  200.3 3.3 %fusion.82 = f32[128,640]{0,1:T(8,128)S(1)} fusion(bf16[1536,128]{1,0:T(8,128)(2,1)} %bitcast.382, bf16[3,1536,640]{2,1,0:T(8,128)(2,1)} %param.13, bf16[4,640,640]{2,1,0:T(8,128)(2,1)} %param.12, bf16[4,640,256]{2,1,0:T(8,128)(2,1)} %param.11), kind=kOutput, calls=%fused_computation.64 | convolution fusion | flops 356761600 | bytes 3670016 | tf_op jit(solution)/shard_map/dot_general | solution.py:69
  206.9 4.0 %fusion.79 = f32[128,640]{0,1:T(8,128)} fusion(bf16[1536,128]{1,0:T(8,128)(2,1)} %bitcast.378, bf16[3,1536,640]{2,1,0:T(8,128)(2,1)} %param.13, bf16[4,640,640]{2,1,0:T(8,128)(2,1)} %param.12, bf16[4,640,256]{2,1,0:T(8,128)(2,1)} %param.11), kind=kOutput, calls=%fused_computation.63 | convolution fusion | flops 356761600 | bytes 3670016 | tf_op jit(solution)/shard_map/dot_general | solution.py:69
  210.9 5.0 %collective-permute-done.21 = bf16[2,1,640,128]{3,2,0,1:T(8,128)(2,1)} collective-permute-done((bf16[2,1,640,128]{3,2,0,1:T(8,128)(2,1)}, bf16[2,1,640,128]{3,2,0,1:T(8,128)(2,1)}, u32[]{:S(2)}, u32[]{:S(2)}) %collective-permute-start.21) | collective-permute-done | bytes 327712 | tf_op jit(solution)/shard_map/ppermute | solution.py:12
  223.5 9.6 %collective-permute-done.22 = bf16[4,1,640,128]{3,2,0,1:T(8,128)(2,1)S(1)} collective-permute-done((bf16[4,1,640,128]{3,2,0,1:T(8,128)(2,1)S(1)}, bf16[4,1,640,128]{3,2,0,1:T(8,128)(2,1)S(1)}, u32[]{:S(2)}, u32[]{:S(2)}) %collective-permute-start.22) | collective-permute-done | bytes 655392 | tf_op jit(solution)/shard_map/ppermute | solution.py:12
  234.8 13.9 %collective-permute-done.10 = bf16[4,1,640,128]{3,2,0,1:T(8,128)(2,1)S(1)} collective-permute-done((bf16[4,1,640,128]{3,2,0,1:T(8,128)(2,1)S(1)}, bf16[4,1,640,128]{3,2,0,1:T(8,128)(2,1)S(1)}, u32[]{:S(2)}, u32[]{:S(2)}) %collective-permute-start.10) | collective-permute-done | bytes 655392 | tf_op jit(solution)/shard_map/ppermute | solution.py:12
  249.6 17.2 %collective-permute-done.23 = bf16[8,640,128]{2,1,0:T(8,128)(2,1)S(1)} collective-permute-done((bf16[8,640,128]{2,1,0:T(8,128)(2,1)S(1)}, bf16[8,640,128]{2,1,0:T(8,128)(2,1)S(1)}, u32[]{:S(2)}, u32[]{:S(2)}) %collective-permute-start.23) | collective-permute-done | bytes 1310752 | tf_op jit(solution)/shard_map/ppermute | solution.py:18
  267.1 3.9 %pad_maximum_fusion.1 = bf16[240,128,128]{2,1,0:T(8,128)(2,1)} fusion(bf16[80,128,128]{2,1,0:T(8,128)(2,1)S(1)} %bitcast.346, bf16[80,128,128]{2,1,0:T(8,128)(2,1)S(1)} %bitcast.345, bf16[80,128,128]{2,1,0:T(8,128)(2,1)S(1)} %bitcast.341), kind=kLoop, calls=%fused_computation.7 | loop fusion | flops 7864320 | bytes 15728640 | tf_op jit(solution)/shard_map/concatenate | solution.py:61
  270.9 21.4 %collective-permute-done.11 = bf16[8,640,128]{2,1,0:T(8,128)(2,1)S(1)} collective-permute-done((bf16[8,640,128]{2,1,0:T(8,128)(2,1)S(1)}, bf16[8,640,128]{2,1,0:T(8,128)(2,1)S(1)}, u32[]{:S(2)}, u32[]{:S(2)}) %collective-permute-start.11) | collective-permute-done | bytes 1310752 | tf_op jit(solution)/shard_map/ppermute | solution.py:18
  292.6 3.8 %pad_maximum_fusion = bf16[240,128,128]{2,1,0:T(8,128)(2,1)} fusion(bf16[80,128,128]{2,1,0:T(8,128)(2,1)S(1)} %bitcast.347, bf16[80,128,128]{2,1,0:T(8,128)(2,1)S(1)} %bitcast.343, bf16[80,128,128]{2,1,0:T(8,128)(2,1)S(1)} %bitcast.338), kind=kLoop, calls=%fused_computation.6 | loop fusion | flops 7864320 | bytes 15728640 | tf_op jit(solution)/shard_map/concatenate | solution.py:61
  296.4 3.9 %gather_fusion.5 = bf16[12,128,128]{2,1,0:T(8,128)(2,1)S(1)} fusion(bf16[240,128,128]{2,1,0:T(8,128)(2,1)} %pad_maximum_fusion.1, s32[1024]{0:T(1024)S(1)} %get-tuple-element.44), kind=kCustom, calls=%fused_computation.5.clone | custom fusion | bytes 786480 | tf_op jit(solution)/shard_map/jit(_take)/gather | solution.py:43
  300.2 3.9 %gather_fusion.2 = bf16[12,128,128]{2,1,0:T(8,128)(2,1)S(1)} fusion(bf16[240,128,128]{2,1,0:T(8,128)(2,1)} %pad_maximum_fusion, s32[1024]{0:T(1024)S(1)} %get-tuple-element.44), kind=kCustom, calls=%fused_computation.2.clone | custom fusion | bytes 786480 | tf_op jit(solution)/shard_map/jit(_take)/gather | solution.py:43
  (132 shorter events, 75.7 us)
Async XLA Ops:
  1.6 2.3 collective-permute-start.12
  3.8 3.2 %collective-permute-start = (bf16[1,1,640,128]{3,2,0,1:T(8,128)(2,1)S(1)}, bf16[1,1,640,128]{3,2,0,1:T(8,128)(2,1)S(1)}, u32[]{:S(2)}, u32[]{:S(2)}) collective-permute-start(bf16[1,1,640,128]{3,2,0,1:T(8,128)(2,1)S(1)} %get-tuple-element.19), channel_id=1, source_target_pairs={{0,1},{1,0},{2,3},{3,2},{4,5},{5,4},{6,7},{7,6},{8,9},{9,8},{10,11... | collective-permute-start | bytes 491528 | tf_op jit(solution)/shard_map/ppermute | solution.py:12
  4.0 11.6 %collective-permute-start.13 = (bf16[2,1,640,128]{3,2,0,1:T(8,128)(2,1)S(1)}, bf16[2,1,640,128]{3,2,0,1:T(8,128)(2,1)S(1)}, u32[]{:S(2)}, u32[]{:S(2)}) collective-permute-start(bf16[2,1,640,128]{3,2,0,1:T(8,128)(2,1)S(1)} %fusion.107), channel_id=1, source_target_pairs={{0,2},{1,3},{2,0},{3,1},{4,6},{5,7},{6,4},{7,5},{8,10},{9,11},{10,... | collective-permute-start | bytes 983048 | tf_op jit(solution)/shard_map/ppermute | solution.py:12
  7.0 14.9 %collective-permute-start.1 = (bf16[2,1,640,128]{3,2,0,1:T(8,128)(2,1)S(1)}, bf16[2,1,640,128]{3,2,0,1:T(8,128)(2,1)S(1)}, u32[]{:S(2)}, u32[]{:S(2)}) collective-permute-start(bf16[2,1,640,128]{3,2,0,1:T(8,128)(2,1)S(1)} %maximum_select_fusion.18), channel_id=1, source_target_pairs={{0,2},{1,3},{2,0},{3,1},{4,6},{5,7},{6,4},{7,5},{8,10},{9,11},{10,... | collective-permute-start | bytes 983048 | tf_op jit(solution)/shard_map/ppermute | solution.py:12
  15.6 17.8 %collective-permute-start.14 = (bf16[4,1,640,128]{3,2,0,1:T(8,128)(2,1)S(1)}, bf16[4,1,640,128]{3,2,0,1:T(8,128)(2,1)}, u32[]{:S(2)}, u32[]{:S(2)}) collective-permute-start(bf16[4,1,640,128]{3,2,0,1:T(8,128)(2,1)S(1)} %maximum_select_fusion.12), channel_id=1, source_target_pairs={{0,4},{1,5},{2,6},{3,7},{4,0},{5,1},{6,2},{7,3},{8,12},{9,13},{10,... | collective-permute-start | bytes 1966088 | tf_op jit(solution)/shard_map/ppermute | solution.py:12
  22.0 23.3 %collective-permute-start.2 = (bf16[4,1,640,128]{3,2,0,1:T(8,128)(2,1)S(1)}, bf16[4,1,640,128]{3,2,0,1:T(8,128)(2,1)}, u32[]{:S(2)}, u32[]{:S(2)}) collective-permute-start(bf16[4,1,640,128]{3,2,0,1:T(8,128)(2,1)S(1)} %maximum_select_fusion.6), channel_id=1, source_target_pairs={{0,4},{1,5},{2,6},{3,7},{4,0},{5,1},{6,2},{7,3},{8,12},{9,13},{10,... | collective-permute-start | bytes 1966088 | tf_op jit(solution)/shard_map/ppermute | solution.py:12
  35.0 33.8 %collective-permute-start.15 = (bf16[8,640,128]{2,1,0:T(8,128)(2,1)S(1)}, bf16[8,640,128]{2,1,0:T(8,128)(2,1)S(1)}, u32[]{:S(2)}, u32[]{:S(2)}) collective-permute-start(bf16[8,640,128]{2,1,0:T(8,128)(2,1)S(1)} %maximum_select_fusion.3), channel_id=1, source_target_pairs={{24,0},{25,1},{26,2},{27,3},{28,4},{29,5},{30,6},{31,7},{0,8},{1,9... | collective-permute-start | bytes 3932168 | tf_op jit(solution)/shard_map/ppermute | solution.py:18
  47.9 43.5 %collective-permute-start.3 = (bf16[8,640,128]{2,1,0:T(8,128)(2,1)}, bf16[8,640,128]{2,1,0:T(8,128)(2,1)}, u32[]{:S(2)}, u32[]{:S(2)}) collective-permute-start(bf16[8,640,128]{2,1,0:T(8,128)(2,1)} %maximum_select_fusion), channel_id=1, source_target_pairs={{24,0},{25,1},{26,2},{27,3},{28,4},{29,5},{30,6},{31,7},{0,8},{1,9... | collective-permute-start | bytes 3932168 | tf_op jit(solution)/shard_map/ppermute | solution.py:18
  99.1 5.6 %collective-permute-start.16 = (bf16[1,1,640,128]{3,2,0,1:T(8,128)(2,1)}, bf16[1,1,640,128]{3,2,0,1:T(8,128)(2,1)S(1)}, u32[]{:S(2)}, u32[]{:S(2)}) collective-permute-start(bf16[1,1,640,128]{3,2,0,1:T(8,128)(2,1)} %get-tuple-element.25), channel_id=1, source_target_pairs={{0,1},{1,0},{2,3},{3,2},{4,5},{5,4},{6,7},{7,6},{8,9},{9,8},{10,11... | collective-permute-start | bytes 491528 | tf_op jit(solution)/shard_map/ppermute | solution.py:12
  104.2 2.6 collective-permute-start.4
  105.7 10.6 %collective-permute-start.17 = (bf16[2,1,640,128]{3,2,0,1:T(8,128)(2,1)S(1)}, bf16[2,1,640,128]{3,2,0,1:T(8,128)(2,1)S(1)}, u32[]{:S(2)}, u32[]{:S(2)}) collective-permute-start(bf16[2,1,640,128]{3,2,0,1:T(8,128)(2,1)S(1)} %fusion.108), channel_id=1, source_target_pairs={{0,2},{1,3},{2,0},{3,1},{4,6},{5,7},{6,4},{7,5},{8,10},{9,11},{10,... | collective-permute-start | bytes 983048 | tf_op jit(solution)/shard_map/ppermute | solution.py:12
  106.9 15.6 %collective-permute-start.5 = (bf16[2,1,640,128]{3,2,0,1:T(8,128)(2,1)S(1)}, bf16[2,1,640,128]{3,2,0,1:T(8,128)(2,1)S(1)}, u32[]{:S(2)}, u32[]{:S(2)}) collective-permute-start(bf16[2,1,640,128]{3,2,0,1:T(8,128)(2,1)S(1)} %fusion.106), channel_id=1, source_target_pairs={{0,2},{1,3},{2,0},{3,1},{4,6},{5,7},{6,4},{7,5},{8,10},{9,11},{10,... | collective-permute-start | bytes 983048 | tf_op jit(solution)/shard_map/ppermute | solution.py:12
  116.5 17.7 %collective-permute-start.18 = (bf16[4,1,640,128]{3,2,0,1:T(8,128)(2,1)S(1)}, bf16[4,1,640,128]{3,2,0,1:T(8,128)(2,1)S(1)}, u32[]{:S(2)}, u32[]{:S(2)}) collective-permute-start(bf16[4,1,640,128]{3,2,0,1:T(8,128)(2,1)S(1)} %maximum_select_fusion.14), channel_id=1, source_target_pairs={{0,4},{1,5},{2,6},{3,7},{4,0},{5,1},{6,2},{7,3},{8,12},{9,13},{10,... | collective-permute-start | bytes 1966088 | tf_op jit(solution)/shard_map/ppermute | solution.py:12
  122.6 22.9 %collective-permute-start.6 = (bf16[4,1,640,128]{3,2,0,1:T(8,128)(2,1)S(1)}, bf16[4,1,640,128]{3,2,0,1:T(8,128)(2,1)S(1)}, u32[]{:S(2)}, u32[]{:S(2)}) collective-permute-start(bf16[4,1,640,128]{3,2,0,1:T(8,128)(2,1)S(1)} %maximum_select_fusion.8), channel_id=1, source_target_pairs={{0,4},{1,5},{2,6},{3,7},{4,0},{5,1},{6,2},{7,3},{8,12},{9,13},{10,... | collective-permute-start | bytes 1966088 | tf_op jit(solution)/shard_map/ppermute | solution.py:12
  134.4 33.5 %collective-permute-start.19 = (bf16[8,640,128]{2,1,0:T(8,128)(2,1)S(1)}, bf16[8,640,128]{2,1,0:T(8,128)(2,1)S(1)}, u32[]{:S(2)}, u32[]{:S(2)}) collective-permute-start(bf16[8,640,128]{2,1,0:T(8,128)(2,1)S(1)} %maximum_select_fusion.4), channel_id=1, source_target_pairs={{24,0},{25,1},{26,2},{27,3},{28,4},{29,5},{30,6},{31,7},{0,8},{1,9... | collective-permute-start | bytes 3932168 | tf_op jit(solution)/shard_map/ppermute | solution.py:18
  145.7 43.9 %collective-permute-start.7 = (bf16[8,640,128]{2,1,0:T(8,128)(2,1)S(1)}, bf16[8,640,128]{2,1,0:T(8,128)(2,1)S(1)}, u32[]{:S(2)}, u32[]{:S(2)}) collective-permute-start(bf16[8,640,128]{2,1,0:T(8,128)(2,1)S(1)} %maximum_select_fusion.1), channel_id=1, source_target_pairs={{24,0},{25,1},{26,2},{27,3},{28,4},{29,5},{30,6},{31,7},{0,8},{1,9... | collective-permute-start | bytes 3932168 | tf_op jit(solution)/shard_map/ppermute | solution.py:18
  203.6 1.5 collective-permute-start.20
  205.9 10.1 %collective-permute-start.21 = (bf16[2,1,640,128]{3,2,0,1:T(8,128)(2,1)}, bf16[2,1,640,128]{3,2,0,1:T(8,128)(2,1)}, u32[]{:S(2)}, u32[]{:S(2)}) collective-permute-start(bf16[2,1,640,128]{3,2,0,1:T(8,128)(2,1)} %fusion.109), channel_id=1, source_target_pairs={{0,2},{1,3},{2,0},{3,1},{4,6},{5,7},{6,4},{7,5},{8,10},{9,11},{10,... | collective-permute-start | bytes 983048 | tf_op jit(solution)/shard_map/ppermute | solution.py:12
  217.1 16.0 %collective-permute-start.22 = (bf16[4,1,640,128]{3,2,0,1:T(8,128)(2,1)S(1)}, bf16[4,1,640,128]{3,2,0,1:T(8,128)(2,1)S(1)}, u32[]{:S(2)}, u32[]{:S(2)}) collective-permute-start(bf16[4,1,640,128]{3,2,0,1:T(8,128)(2,1)S(1)} %maximum_select_fusion.16), channel_id=1, source_target_pairs={{0,4},{1,5},{2,6},{3,7},{4,0},{5,1},{6,2},{7,3},{8,12},{9,13},{10,... | collective-permute-start | bytes 1966088 | tf_op jit(solution)/shard_map/ppermute | solution.py:12
  219.2 1.5 collective-permute-start.8
  220.7 12.7 %collective-permute-start.9 = (bf16[2,1,640,128]{3,2,0,1:T(8,128)(2,1)S(1)}, bf16[2,1,640,128]{3,2,0,1:T(8,128)(2,1)S(1)}, u32[]{:S(2)}, u32[]{:S(2)}) collective-permute-start(bf16[2,1,640,128]{3,2,0,1:T(8,128)(2,1)S(1)} %maximum_select_fusion.21), channel_id=1, source_target_pairs={{0,2},{1,3},{2,0},{3,1},{4,6},{5,7},{6,4},{7,5},{8,10},{9,11},{10,... | collective-permute-start | bytes 983048 | tf_op jit(solution)/shard_map/ppermute | solution.py:12
  233.3 33.5 %collective-permute-start.23 = (bf16[8,640,128]{2,1,0:T(8,128)(2,1)S(1)}, bf16[8,640,128]{2,1,0:T(8,128)(2,1)S(1)}, u32[]{:S(2)}, u32[]{:S(2)}) collective-permute-start(bf16[8,640,128]{2,1,0:T(8,128)(2,1)S(1)} %maximum_select_fusion.5), channel_id=1, source_target_pairs={{24,0},{25,1},{26,2},{27,3},{28,4},{29,5},{30,6},{31,7},{0,8},{1,9... | collective-permute-start | bytes 3932168 | tf_op jit(solution)/shard_map/ppermute | solution.py:18
  233.6 15.1 %collective-permute-start.10 = (bf16[4,1,640,128]{3,2,0,1:T(8,128)(2,1)S(1)}, bf16[4,1,640,128]{3,2,0,1:T(8,128)(2,1)S(1)}, u32[]{:S(2)}, u32[]{:S(2)}) collective-permute-start(bf16[4,1,640,128]{3,2,0,1:T(8,128)(2,1)S(1)} %maximum_select_fusion.10), channel_id=1, source_target_pairs={{0,4},{1,5},{2,6},{3,7},{4,0},{5,1},{6,2},{7,3},{8,12},{9,13},{10,... | collective-permute-start | bytes 1966088 | tf_op jit(solution)/shard_map/ppermute | solution.py:12
  248.9 43.5 %collective-permute-start.11 = (bf16[8,640,128]{2,1,0:T(8,128)(2,1)S(1)}, bf16[8,640,128]{2,1,0:T(8,128)(2,1)S(1)}, u32[]{:S(2)}, u32[]{:S(2)}) collective-permute-start(bf16[8,640,128]{2,1,0:T(8,128)(2,1)S(1)} %maximum_select_fusion.2), channel_id=1, source_target_pairs={{24,0},{25,1},{26,2},{27,3},{28,4},{29,5},{30,6},{31,7},{0,8},{1,9... | collective-permute-start | bytes 3932168 | tf_op jit(solution)/shard_map/ppermute | solution.py:18
  (17 other events, 148.0 us)
where the time goes:
time: 313 us; the launch traced here: 312 us
  waiting for transfers between devices  212 us (68%)
  other arithmetic  36.4 us (12%)
  matrix products  23.9 us (8%)
  starting transfers between devices  22.4 us (7%)
  local copies, waits for them, and re-layouts  16.8 us (5%)
    ppermute x6, waiting for transfers between devices, shifted(): return lax.ppermute(block, axis, route)  117 us
    ppermute x18, waiting for transfers between devices, swapped(): lax.ppermute(shard, axis, [(i, i ^ 1 << stride) for i in range(lax.axis_s...  95 us
    dot_general x8, matrix products, solve_columns(): jnp.dot(inv_diag[height_index], rounded, preferred_element_type=jnp.float32)  23.9 us
    ppermute x18, starting transfers between devices, swapped(): lax.ppermute(shard, axis, [(i, i ^ 1 << stride) for i in range(lax.axis_s...  18.4 us
    gather x6, local copies, waits for them, and re-layouts, subtract(): picked = jnp.take(pool, indices, axis=0)  15.2 us
    concatenate x4, other arithmetic, solve_columns(): pool = jnp.concatenate(pooled, 0)  13.8 us
    select_n x29, other arithmetic, gather_group(): jnp.where(upper_half, jnp.concatenate([partner, gathered], 0), jnp.concat...  10.5 us
  transfers between devices with their start and end apart: 24, of which 19 were waited for; matrix products, arithmetic and copies ran while one was open for 10% of the time, Pallas kernels for 0%

commit v1 on v0

v1 whole, which is shorter than its diff:
```python
import functools

import jax
import jax.numpy as jnp
from jax import lax
from jax.experimental import pallas as pl
from jax.experimental.pallas import tpu as pltpu
from jax.sharding import PartitionSpec as P

GROUP = 8
CORES = 2
CHIPS = GROUP // CORES


HBM = pl.BlockSpec(memory_space=pltpu.HBM)
VMEM = pl.BlockSpec(memory_space=pltpu.VMEM)
SMEM = pl.BlockSpec(memory_space=pltpu.SMEM)
PARAMS = pltpu.CompilerParams(vmem_limit_bytes=16 * 2**20)


LATE = (2, 3)
ORDER = tuple(hop for hop in range(CHIPS) if hop not in LATE) + LATE


def send(value, hop, step=0):
    size = lax.axis_size("nodes")
    route = [(i, ((i ^ (hop * CORES)) + step * GROUP) % size) for i in range(size)]
    return lax.ppermute(value, "nodes", route)


def swap(value):
    size = lax.axis_size("nodes")
    return lax.ppermute(value, "nodes", [(i, i ^ 1) for i in range(size)])


def call(kernel, out_shape, in_specs, out_specs, flops, moved, scratch=(), aliases=None):
    return pl.pallas_call(
        kernel,
        out_shape=out_shape,
        in_specs=in_specs,
        out_specs=out_specs,
        scratch_shapes=list(scratch),
        input_output_aliases=aliases or {},
        compiler_params=PARAMS,
        cost_estimate=pl.CostEstimate(flops=flops, bytes_accessed=moved, transcendentals=0),
    )


def chip_place():
    return lax.axis_index("nodes") % GROUP // CORES


def run_copies(copies):
    for copy in copies:
        copy.start()
    for copy in copies:
        copy.wait()


def solve_rows(inv_ref, reduced_ref, x_ref, piece_refs, tile, row_done=None):
    width = inv_ref.shape[0]
    quarter = tile // CHIPS
    per_node = width // tile
    for i in reversed(range(per_node)):
        x_ref[i * tile : (i + 1) * tile, :] = jnp.dot(
            inv_ref[i * tile : (i + 1) * tile, i * tile :],
            reduced_ref[i * tile :, :],
            preferred_element_type=jnp.float32,
        )
        if row_done is not None:
            row_done(i)
    for relative, piece_ref in enumerate(piece_refs):
        first = (chip_place() ^ relative) * quarter
        for i in range(per_node):
            start = pl.multiple_of(i * tile + first, quarter)
            piece_ref[i] = x_ref[pl.ds(start, quarter), :].astype(jnp.bfloat16)


def first_kernel(tile, list_ref, rhs_hbm, inv_hbm, x_ref, *refs):
    piece_refs, noted_refs = refs[:CHIPS], refs[CHIPS:-4]
    rhs_ref, inv_ref, note_ref, sems = refs[-4:]
    copies = [
        pltpu.make_async_copy(rhs_hbm.at[0], rhs_ref, sems.at[0]),
        pltpu.make_async_copy(inv_hbm.at[0], inv_ref, sems.at[1]),
    ]
    for copy in copies:
        copy.start()
    levels, _, slots = list_ref.shape
    note_ref[...] = jnp.zeros_like(note_ref)
    for level in range(levels):
        note_ref[level : level + 1, :slots] = list_ref[level].astype(jnp.float32)
    note = note_ref[...].astype(jnp.bfloat16)
    for copy in copies:
        copy.wait()
    solve_rows(inv_ref, rhs_ref, x_ref, piece_refs, tile)
    for piece_ref, noted_ref in zip(piece_refs[1:], noted_refs):
        per_node = piece_ref.shape[0]
        noted_ref[:per_node] = piece_ref[...]
        noted_ref[per_node] = note


def load_kernel(level, after_ref, rhs_hbm, inv_hbm, factor_hbm, rhs_ref, inv_ref, turned_ref, *scratch):
    factor_ref, sems = scratch
    copies = [
        pltpu.make_async_copy(
            factor_hbm.at[level - 1, :, chip_place() ^ relative],
            factor_ref.at[place],
            sems.at[place],
        )
        for place, relative in enumerate(ORDER)
    ] + [
        pltpu.make_async_copy(rhs_hbm.at[level], rhs_ref, sems.at[CHIPS]),
        pltpu.make_async_copy(inv_hbm.at[level], inv_ref, sems.at[CHIPS + 1]),
    ]
    for copy in copies:
        copy.start()
    for relative in range(CHIPS):
        copies[relative].wait()
        slots, quarter, width = factor_ref.shape[1:]
        depth = slots * quarter
        turned_ref[:, relative * depth : (relative + 1) * depth] = (
            factor_ref[relative].reshape(depth, width).T
        )
    for copy in copies[CHIPS:]:
        copy.wait()


def store_kernel(level, x_ref, *refs):
    out_hbm, sem = refs[-2:]
    run_copies([pltpu.make_async_copy(x_ref, out_hbm.at[level], sem)])


def live_part(level, count_ref, part_ref):
    slots, quarter, columns = part_ref.shape
    count = count_ref[:, level - 1 : level]
    part = part_ref[...].reshape(slots * quarter, columns)
    slot_row = lax.broadcasted_iota(jnp.int32, part.shape, 0)
    return jnp.where(slot_row < count * quarter, part, jnp.zeros_like(part))


def less_update(level, relatives, count_ref, base_ref, turned_ref, part_refs, joined_ref, out_ref):
    depth = joined_ref.shape[0] // len(relatives)
    for index, part_ref in enumerate(part_refs):
        joined_ref[index * depth : (index + 1) * depth, :] = live_part(
            level, count_ref, part_ref
        )
    first = ORDER.index(relatives[0]) * depth
    update = jnp.dot(
        turned_ref[:, first : first + joined_ref.shape[0]],
        joined_ref[...],
        preferred_element_type=jnp.float32,
    )
    out_ref[...] = (base_ref[...].astype(jnp.float32) - update).astype(out_ref.dtype)


def update_kernel(level, relatives, count_ref, base_ref, turned_ref, *refs):
    parts, (out_ref, joined_ref) = refs[:-2], refs[-2:]
    less_update(
        level, relatives, count_ref, base_ref, turned_ref, parts, joined_ref, out_ref
    )


def level_kernel(level, levels, tile, relatives, count_ref, base_ref, inv_ref, turned_ref, *refs):
    last = level == levels - 1
    parts, refs = refs[: len(relatives)], refs[len(relatives) :]
    joined_ref, reduced_ref = refs[-2:]
    refs = refs[:-1]
    less_update(
        level, relatives, count_ref, base_ref, turned_ref, parts, joined_ref, reduced_ref
    )
    if not last:
        solve_rows(inv_ref, reduced_ref, refs[0], refs[1:-1], tile)
        return
    out_hbm, x_ref, sems = refs[1:-1]

    def row_copy(i):
        rows = pl.ds(i * tile, tile)
        return pltpu.make_async_copy(x_ref.at[rows], out_hbm.at[level, rows], sems.at[i])

    solve_rows(inv_ref, reduced_ref, x_ref, (), tile, lambda i: row_copy(i).start())
    for i in range(inv_ref.shape[0] // tile):
        row_copy(i).wait()


def select_kernel(level, last, places_ref, *refs):
    old, fresh = refs[: level - 1], refs[level - 1 : -CHIPS - 1]
    pool_ref, outs = (refs[-1], refs[-CHIPS - 1 : -1]) if last else (refs[-CHIPS - 1], refs[-CHIPS:])
    step = pool_ref.shape[0] // len(fresh)
    for place, ref in enumerate(fresh):
        pool_ref[place * step : (place + 1) * step] = ref[:step]
    size = pool_ref.shape[0]
    slots = outs[0].shape[0]
    named = places_ref[level - 1 : level, :]
    for relative, out_ref in enumerate(outs):
        for slot in range(slots):
            place = named[0, relative * slots + slot]
            if level == 1:
                out_ref[slot] = pool_ref[place]
                continue
            value = None
            for index, pool in enumerate(old + (pool_ref,)):
                local = place - index * size
                found = pool[jnp.clip(local, 0, size - 1)]
                value = found if value is None else jnp.where(local >= 0, found, value)
            out_ref[slot] = value


def body(rhs, inv_diag, factor, tile_list, live_count):
    levels, width, columns = rhs.shape
    slots = tile_list.shape[2]
    tile = factor.shape[1] // slots
    per_node = width // tile
    quarter = tile // CHIPS
    pool = 2 * GROUP * per_node
    half = jnp.bfloat16
    piece = jax.ShapeDtypeStruct((per_node, quarter, columns), half)
    solved = jax.ShapeDtypeStruct((width, columns), jnp.float32)
    part = jax.ShapeDtypeStruct((slots, quarter, columns), half)
    out_shape = jax.ShapeDtypeStruct((levels, width, columns), jnp.float32)
    solve_flops = width * width * columns
    part_flops = 2 * slots * quarter * width * columns
    part_moved = 2 * slots * quarter * (width + columns) + 8 * width * columns
    semaphores = pltpu.SemaphoreType.DMA

    rhs, inv_diag, factor = (
        pltpu.with_memory_space_constraint(value, pltpu.HBM)
        for value in (rhs, inv_diag, factor.reshape(-1, slots, CHIPS, quarter, width))
    )

    assert (levels - 1) * pool <= 256 and levels - 1 <= quarter and slots <= columns
    shapes = (solved,) + (piece,) * CHIPS
    noted = jax.ShapeDtypeStruct((per_node + 1, quarter, columns), half)
    solution, *outputs = call(
        functools.partial(first_kernel, tile),
        shapes + (noted,) * (CHIPS - 1),
        [VMEM, HBM, HBM],
        [VMEM] * (len(shapes) + CHIPS - 1),
        solve_flops,
        2 * width * (width + 4 * columns),
        [
            pltpu.VMEM((width, columns), half),
            pltpu.VMEM((width, width), half),
            pltpu.VMEM((quarter, columns), jnp.float32),
            semaphores((2,)),
        ],
    )(tile_list, rhs, inv_diag)
    pieces, noted = outputs[:CHIPS], outputs[CHIPS:]

    position = lax.axis_index("nodes") % GROUP
    chip, core = position // CORES, position % CORES
    own = [pieces[0]] + [send(value, hop) for hop, value in zip(range(1, CHIPS), noted)]
    notes = [value[per_node, : levels - 1, :slots] for value in [noted[0]] + own[1:]]
    lists = jnp.stack(notes, 1).astype(jnp.int32)
    named, inside = lists // pool, lists % pool
    group, inside = inside // (GROUP * per_node), inside % (GROUP * per_node)
    member, row = inside // per_node, inside % per_node
    side = 2 * group + ((member % CORES) ^ core)
    places = named * pool + (side * CHIPS + ((member // CORES) ^ chip)) * per_node + row
    places = places.reshape(levels - 1, CHIPS * slots)
    counts = live_count.T

    pools = []
    for level in range(1, levels):
        last = level == levels - 1
        previous = [send(pieces[hop], hop, 1) for hop in range(CHIPS)]
        if level > 1:
            own = [pieces[0]] + [send(pieces[hop], hop) for hop in range(1, CHIPS)]
        rhs_here, inv_here, turned = call(
            functools.partial(load_kernel, level),
            (
                jax.ShapeDtypeStruct((width, columns), half),
                jax.ShapeDtypeStruct((width, width), half),
                jax.ShapeDtypeStruct((width, slots * tile), half),
            ),
            [HBM] * 4,
            [VMEM] * 3,
            0,
            2 * width * (columns + width + slots * tile),
            [pltpu.VMEM((CHIPS, slots, quarter, width), half), semaphores((2 + CHIPS,))],
        )(pieces[0], rhs, inv_diag, factor)
        out = call(
            functools.partial(store_kernel, level - 1),
            out_shape,
            [VMEM] if level == 1 else [VMEM, HBM],
            HBM,
            0,
            4 * width * columns,
            [semaphores],
            {} if level == 1 else {1: 0},
        )(*((solution,) if level == 1 else (solution, out)))
        fresh = previous + [swap(value) for value in previous] + own + [swap(value) for value in own]

        inputs = pools + fresh
        packed = jax.ShapeDtypeStruct((pool, quarter, columns), half)
        selected = call(
            functools.partial(select_kernel, level, last),
            (part,) * CHIPS if last else (packed,) + (part,) * CHIPS,
            [VMEM] * (1 + len(inputs)),
            [VMEM] * (CHIPS if last else 1 + CHIPS),
            0,
            4 * (slots * CHIPS + pool) * quarter * columns,
            [pltpu.VMEM(packed.shape, half)] if last else [],
        )(places, *inputs)
        pools, parts = pools + list(selected[:-CHIPS]), selected[-CHIPS:]
        parts = [parts[0]] + [send(parts[hop], hop) for hop in range(1, CHIPS)]
        late = LATE
        early = tuple(hop for hop in range(CHIPS) if hop not in late)
        base = call(
            functools.partial(update_kernel, level, early),
            solved,
            [VMEM] * (3 + len(early)),
            VMEM,
            part_flops * len(early),
            part_moved * len(early),
            [pltpu.VMEM((len(early) * slots * quarter, columns), half)],
        )(counts, rhs_here, turned, *[parts[hop] for hop in early])
        level_call = functools.partial(
            call,
            functools.partial(level_kernel, level, levels, tile, late),
            flops=solve_flops + part_flops * len(late),
            moved=part_moved * len(late),
        )
        operands = (counts, base, inv_here, turned) + tuple(parts[hop] for hop in late)
        in_specs = [VMEM] * len(operands)
        joined = pltpu.VMEM((len(late) * slots * quarter, columns), half)
        reduced = pltpu.VMEM((width, columns), half)
        if last:
            return level_call(
                out_shape=out_shape,
                in_specs=in_specs + [HBM],
                out_specs=HBM,
                scratch=[pltpu.VMEM((width, columns), jnp.float32), semaphores((per_node,)), joined, reduced],
                aliases={len(operands): 0},
            )(*operands, out)
        solution, *pieces = level_call(
            out_shape=shapes,
            in_specs=in_specs,
            out_specs=[VMEM] * len(shapes),
            scratch=[joined, reduced],
        )(*operands)


def solution(mesh):
    return jax.shard_map(
        body,
        mesh=mesh,
        in_specs=(
            P(None, "nodes", None),
            P(None, "nodes", None),
            P(None, "nodes", None),
            P(None, "nodes", None),
            P(None, "nodes"),
        ),
        out_specs=P(None, "nodes", None),
        check_vma=False,
    )
```

time: 313 us -> 99.2 us (0.32)
  waiting for transfers between devices: 212 us -> 35.2 us
  other arithmetic: 36.4 us -> 0.08 us
  matrix products: 23.9 us -> 0 us
  starting transfers between devices: 22.4 us -> 46.1 us
  Pallas kernels: 0 us -> 16.3 us
  local copies, waits for them, and re-layouts: 16.8 us -> 0.97 us
    ppermute x24 -> x54, waiting for transfers between devices: 212 us -> 35.2 us  [the longest x30 32.1 us: send(): return lax.ppermute(value, 'nodes', route)]
    dot_general x8 -> x0, matrix products: 23.9 us -> none  [solve_columns(): jnp.dot(inv_diag[height_index], rounded, preferred_element_type=jnp.float32)]
    ppermute x24 -> x54, starting transfers between devices: 22.4 us -> 46.1 us  [the longest x30 42.8 us: send(): return lax.ppermute(value, 'nodes', route)]
    concatenate x15 -> x0, other arithmetic: 18.7 us -> none  [the longest x4 13.8 us: solve_columns(): pool = jnp.concatenate(pooled, 0)]
    pallas_call x0 -> x16, Pallas kernels: none -> 16.3 us  [the longest x3 5.7 us: body(): call(functools.partial(load_kernel, level), (jax.ShapeDtypeStruct((width,...]
    gather x6 -> x0, local copies, waits for them, and re-layouts: 15.2 us -> none  [subtract(): picked = jnp.take(pool, indices, axis=0)]
    select_n x32 -> x0, other arithmetic: 12.8 us -> none  [the longest x29 10.5 us: gather_group(): jnp.where(upper_half, jnp.concatenate([partner, gathered], 0), jnp.concat...]
  transfers between devices with their start and end apart: 24 -> 54, of which waited for: 19 -> 29; matrix products, arithmetic and copies ran while one was open for 10% -> 0% of each run, Pallas kernels for 0% -> 10%
where the time goes in v1:
time: 99.2 us; the launch traced here: 98.9 us
  starting transfers between devices  46.1 us (46%)
  waiting for transfers between devices  35.2 us (35%)
  Pallas kernels  16.3 us (16%)
    ppermute x30, starting transfers between devices, send(): return lax.ppermute(value, 'nodes', route)  42.8 us
    ppermute x30, waiting for transfers between devices, send(): return lax.ppermute(value, 'nodes', route)  32.1 us
    pallas_call x3, Pallas kernels, body(): call(functools.partial(load_kernel, level), (jax.ShapeDtypeStruct((width,...  5.7 us
    ppermute x24, starting transfers between devices, swap(): return lax.ppermute(value, 'nodes', [(i, i ^ 1) for i in range(size)])  3.29 us
    ppermute x24, waiting for transfers between devices, swap(): return lax.ppermute(value, 'nodes', [(i, i ^ 1) for i in range(size)])  3.02 us
    pallas_call x3, Pallas kernels, body(): call(functools.partial(store_kernel, level - 1), out_shape, [VMEM] if lev...  2.54 us
    pallas_call x2, Pallas kernels, body(): level_call(out_shape=shapes, in_specs=in_specs, out_specs=[VMEM] * len(sh...  2.19 us
  transfers between devices with their start and end apart: 54, of which 29 were waited for; matrix products, arithmetic and copies ran while one was open for 0% of the time, Pallas kernels for 10%

profile of v1, /device:TPU:0, one launch (start us, length us, event | category | flops | bytes accessed | tf_op | source)
XLA Modules:
  0.0 98.9 jit_solution(15170839250567704101)
XLA Ops:
  0.7 1.6 %shard_map.55 = (f32[640,256]{1,0:T(8,128)S(1)}, bf16[5,32,256]{2,1,0:T(8,128)(2,1)S(1)}, bf16[5,32,256]{2,1,0:T(8,128)(2,1)S(1)}, bf16[5,32,256]{2,1,0:T(8,128)...) custom-call(s32[3,1,12]{2,1,0:T(1,128)S(1)} %copy-done.1, ...), custom_call_target="tpu_custom_call" | custom-call | flops 104857600 | bytes 2129920 | tf_op jit(solution)/shard_map/pallas_call | solution.py:233
  2.3 3.0 %collective-permute-start = (bf16[6,32,256]{2,1,0:T(8,128)(2,1)S(1)}, bf16[6,32,256]{2,1,0:T(8,128)(2,1)S(1)}, u32[]{:S(2)}, u32[]{:S(2)}) collective-permute-start(bf16[6,32,256]{2,1,0:T(8,128)(2,1)S(1)} %get-tuple-element.49), channel_id=1, source_target_pairs={{0,2},{1,3},{2,0},{3,1},{4,6},{5,7},{6,4},{7,5},{8,10},{9,11},{10,... | collective-permute-start | bytes 294920 | tf_op jit(solution)/shard_map/ppermute | solution.py:28
  5.3 1.5 %collective-permute-start.1 = (bf16[6,32,256]{2,1,0:T(8,128)(2,1)S(1)}, bf16[6,32,256]{2,1,0:T(8,128)(2,1)S(1)}, u32[]{:S(2)}, u32[]{:S(2)}) collective-permute-start(bf16[6,32,256]{2,1,0:T(8,128)(2,1)S(1)} %get-tuple-element.50), channel_id=1, source_target_pairs={{0,4},{1,5},{2,6},{3,7},{4,0},{5,1},{6,2},{7,3},{8,12},{9,13},{10,... | collective-permute-start | bytes 294920 | tf_op jit(solution)/shard_map/ppermute | solution.py:28
  6.9 2.0 %collective-permute-start.3 = (bf16[5,32,256]{2,1,0:T(8,128)(2,1)S(1)}, bf16[5,32,256]{2,1,0:T(8,128)(2,1)S(1)}, u32[]{:S(2)}, u32[]{:S(2)}) collective-permute-start(bf16[5,32,256]{2,1,0:T(8,128)(2,1)S(1)} %get-tuple-element.46.after_ref.refs_8_), channel_id=1, source_target_pairs={{0,8},{1,9},{2,10},{3,11},{4,12},{5,13},{6,14},{7,15},{8,16},{9,17... | collective-permute-start | bytes 245768 | tf_op jit(solution)/shard_map/ppermute | solution.py:28
  8.9 3.5 %collective-permute-start.6 = (bf16[5,32,256]{2,1,0:T(8,128)(2,1)S(1)}, bf16[5,32,256]{2,1,0:T(8,128)(2,1)S(1)}, u32[]{:S(2)}, u32[]{:S(2)}) collective-permute-start(bf16[5,32,256]{2,1,0:T(8,128)(2,1)S(1)} %get-tuple-element.54), channel_id=1, source_target_pairs={{0,14},{1,15},{2,12},{3,13},{4,10},{5,11},{6,8},{7,9},{8,22},{9,23... | collective-permute-start | bytes 245768 | tf_op jit(solution)/shard_map/ppermute | solution.py:28
  12.4 1.6 %collective-permute-start.4 = (bf16[5,32,256]{2,1,0:T(8,128)(2,1)S(1)}, bf16[5,32,256]{2,1,0:T(8,128)(2,1)S(1)}, u32[]{:S(2)}, u32[]{:S(2)}) collective-permute-start(bf16[5,32,256]{2,1,0:T(8,128)(2,1)S(1)} %get-tuple-element.52), channel_id=1, source_target_pairs={{0,10},{1,11},{2,8},{3,9},{4,14},{5,15},{6,12},{7,13},{8,18},{9,19... | collective-permute-start | bytes 245768 | tf_op jit(solution)/shard_map/ppermute | solution.py:28
  14.4 3.5 %collective-permute-done.6.refs_3_ = bf16[5,32,256]{2,1,0:T(8,128)(2,1)S(1)} collective-permute-done((bf16[5,32,256]{2,1,0:T(8,128)(2,1)S(1)}, bf16[5,32,256]{2,1,0:T(8,128)(2,1)S(1)}, u32[]{:S(2)}, u32[]{:S(2)}) %collective-permute-start.6) | collective-permute-done | bytes 81952 | tf_op jit(solution)/shard_map/ppermute | solution.py:28
  17.9 1.7 %collective-permute-done.4.refs_1_ = bf16[5,32,256]{2,1,0:T(8,128)(2,1)S(1)} collective-permute-done((bf16[5,32,256]{2,1,0:T(8,128)(2,1)S(1)}, bf16[5,32,256]{2,1,0:T(8,128)(2,1)S(1)}, u32[]{:S(2)}, u32[]{:S(2)}) %collective-permute-start.4) | collective-permute-done | bytes 81952 | tf_op jit(solution)/shard_map/ppermute | solution.py:28
  19.6 1.5 %collective-permute-done.5.refs_2_ = bf16[5,32,256]{2,1,0:T(8,128)(2,1)S(1)} collective-permute-done((bf16[5,32,256]{2,1,0:T(8,128)(2,1)S(1)}, bf16[5,32,256]{2,1,0:T(8,128)(2,1)S(1)}, u32[]{:S(2)}, u32[]{:S(2)}) %collective-permute-start.5) | collective-permute-done | bytes 81952 | tf_op jit(solution)/shard_map/ppermute | solution.py:28
  24.0 1.6 %collective-permute-start.15 = (bf16[12,32,256]{2,1,0:T(8,128)(2,1)S(1)}, bf16[12,32,256]{2,1,0:T(8,128)(2,1)S(1)}, u32[]{:S(2)}, u32[]{:S(2)}) collective-permute-start(bf16[12,32,256]{2,1,0:T(8,128)(2,1)S(1)} %get-tuple-element.56), channel_id=1, source_target_pairs={{0,2},{1,3},{2,0},{3,1},{4,6},{5,7},{6,4},{7,5},{8,10},{9,11},{10,... | collective-permute-start | bytes 589832 | tf_op jit(solution)/shard_map/ppermute | solution.py:28
  26.1 1.5 %collective-permute-start.17 = (bf16[12,32,256]{2,1,0:T(8,128)(2,1)S(1)}, bf16[12,32,256]{2,1,0:T(8,128)(2,1)S(1)}, u32[]{:S(2)}, u32[]{:S(2)}) collective-permute-start(bf16[12,32,256]{2,1,0:T(8,128)(2,1)S(1)} %get-tuple-element.59), channel_id=1, source_target_pairs={{0,6},{1,7},{2,4},{3,5},{4,2},{5,3},{6,0},{7,1},{8,14},{9,15},{10,... | collective-permute-start | bytes 589832 | tf_op jit(solution)/shard_map/ppermute | solution.py:28
  27.6 1.9 %shard_map.56 = (bf16[640,256]{1,0:T(8,128)(2,1)S(1)}, bf16[640,640]{1,0:T(8,128)(2,1)S(1)}, bf16[640,1536]{1,0:T(8,128)(2,1)S(1)}) custom-call(bf16[5,32,256]{2,1,0:T(8,128)(2,1)S(1)} %get-tuple-element.46.after_ref.refs_8_, bf16[4,640,256]{2,1,0:T(8,128)(2,1)} %rhs_hbm.7, bf16[4,640,640]{2,1,0:T(8,128)(2,1)} %inv_hbm.7, bf16[3,12,4,32,640]{4,3,2,1,0:T(8,128)(2,1)} %bitcast.16), custom_call_target="tpu_custom_call" | custom-call | bytes 3112960 | tf_op jit(solution)/shard_map/pallas_call | solution.py:268
  29.5 2.4 %collective-permute-done.15.refs_1_ = bf16[12,32,256]{2,1,0:T(8,128)(2,1)S(1)} collective-permute-done((bf16[12,32,256]{2,1,0:T(8,128)(2,1)S(1)}, bf16[12,32,256]{2,1,0:T(8,128)(2,1)S(1)}, u32[]{:S(2)}, u32[]{:S(2)}) %collective-permute-start.15) | collective-permute-done | bytes 196640 | tf_op jit(solution)/shard_map/ppermute | solution.py:28
  32.3 4.1 %collective-permute-done.16.refs_0_ = bf16[12,32,256]{2,1,0:T(8,128)(2,1)S(1)} collective-permute-done((bf16[12,32,256]{2,1,0:T(8,128)(2,1)S(1)}, bf16[12,32,256]{2,1,0:T(8,128)(2,1)S(1)}, u32[]{:S(2)}, u32[]{:S(2)}) %collective-permute-start.16) | collective-permute-done | bytes 196640 | tf_op jit(solution)/shard_map/ppermute | solution.py:28
  37.7 2.4 %collective-permute-start.20 = (bf16[5,32,256]{2,1,0:T(8,128)(2,1)S(1)}, bf16[5,32,256]{2,1,0:T(8,128)(2,1)S(1)}, u32[]{:S(2)}, u32[]{:S(2)}) collective-permute-start(bf16[5,32,256]{2,1,0:T(8,128)(2,1)S(1)} %get-tuple-element.65), channel_id=1, source_target_pairs={{0,12},{1,13},{2,14},{3,15},{4,8},{5,9},{6,10},{7,11},{8,20},{9,21... | collective-permute-start | bytes 245768 | tf_op jit(solution)/shard_map/ppermute | solution.py:28
  40.1 4.2 %collective-permute-start.21 = (bf16[5,32,256]{2,1,0:T(8,128)(2,1)S(1)}, bf16[5,32,256]{2,1,0:T(8,128)(2,1)S(1)}, u32[]{:S(2)}, u32[]{:S(2)}) collective-permute-start(bf16[5,32,256]{2,1,0:T(8,128)(2,1)S(1)} %get-tuple-element.66), channel_id=1, source_target_pairs={{0,14},{1,15},{2,12},{3,13},{4,10},{5,11},{6,8},{7,9},{8,22},{9,23... | collective-permute-start | bytes 245768 | tf_op jit(solution)/shard_map/ppermute | solution.py:28
  57.7 1.9 %shard_map.60 = (bf16[640,256]{1,0:T(8,128)(2,1)S(1)}, bf16[640,640]{1,0:T(8,128)(2,1)S(1)}, bf16[640,1536]{1,0:T(8,128)(2,1)S(1)}) custom-call(bf16[5,32,256]{2,1,0:T(8,128)(2,1)S(1)} %get-tuple-element.60.after_ref.refs_9_, bf16[4,640,256]{2,1,0:T(8,128)(2,1)} %rhs_hbm.7, bf16[4,640,640]{2,1,0:T(8,128)(2,1)} %inv_hbm.7, bf16[3,12,4,32,640]{4,3,2,1,0:T(8,128)(2,1)} %bitcast.17), custom_call_target="tpu_custom_call" | custom-call | bytes 3112960 | tf_op jit(solution)/shard_map/pallas_call | solution.py:268
  59.6 2.4 %collective-permute-done.33.refs_1_ = bf16[12,32,256]{2,1,0:T(8,128)(2,1)S(1)} collective-permute-done((bf16[12,32,256]{2,1,0:T(8,128)(2,1)S(1)}, bf16[12,32,256]{2,1,0:T(8,128)(2,1)S(1)}, u32[]{:S(2)}, u32[]{:S(2)}) %collective-permute-start.33) | collective-permute-done | bytes 196640 | tf_op jit(solution)/shard_map/ppermute | solution.py:28
  62.5 4.2 %collective-permute-done.34.refs_0_ = bf16[12,32,256]{2,1,0:T(8,128)(2,1)S(1)} collective-permute-done((bf16[12,32,256]{2,1,0:T(8,128)(2,1)S(1)}, bf16[12,32,256]{2,1,0:T(8,128)(2,1)S(1)}, u32[]{:S(2)}, u32[]{:S(2)}) %collective-permute-start.34) | collective-permute-done | bytes 196640 | tf_op jit(solution)/shard_map/ppermute | solution.py:28
  68.2 1.7 %collective-permute-start.38 = (bf16[5,32,256]{2,1,0:T(8,128)(2,1)S(1)}, bf16[5,32,256]{2,1,0:T(8,128)(2,1)S(1)}, u32[]{:S(2)}, u32[]{:S(2)}) collective-permute-start(bf16[5,32,256]{2,1,0:T(8,128)(2,1)S(1)} %get-tuple-element.77), channel_id=1, source_target_pairs={{0,12},{1,13},{2,14},{3,15},{4,8},{5,9},{6,10},{7,11},{8,20},{9,21... | collective-permute-start | bytes 245768 | tf_op jit(solution)/shard_map/ppermute | solution.py:28
  69.9 4.6 %collective-permute-start.39 = (bf16[5,32,256]{2,1,0:T(8,128)(2,1)S(1)}, bf16[5,32,256]{2,1,0:T(8,128)(2,1)S(1)}, u32[]{:S(2)}, u32[]{:S(2)}) collective-permute-start(bf16[5,32,256]{2,1,0:T(8,128)(2,1)S(1)} %get-tuple-element.78), channel_id=1, source_target_pairs={{0,14},{1,15},{2,12},{3,13},{4,10},{5,11},{6,8},{7,9},{8,22},{9,23... | collective-permute-start | bytes 245768 | tf_op jit(solution)/shard_map/ppermute | solution.py:28
  89.9 1.9 %shard_map.64 = (bf16[640,256]{1,0:T(8,128)(2,1)S(1)}, bf16[640,640]{1,0:T(8,128)(2,1)S(1)}, bf16[640,1536]{1,0:T(8,128)(2,1)S(1)}) custom-call(bf16[5,32,256]{2,1,0:T(8,128)(2,1)S(1)} %get-tuple-element.72.after_ref.refs_10_, bf16[4,640,256]{2,1,0:T(8,128)(2,1)} %rhs_hbm.7, bf16[4,640,640]{2,1,0:T(8,128)(2,1)} %inv_hbm.7, bf16[3,12,4,32,640]{4,3,2,1,0:T(8,128)(2,1)} %bitcast.18), custom_call_target="tpu_custom_call" | custom-call | bytes 3112960 | tf_op jit(solution)/shard_map/pallas_call | solution.py:268
  93.2 3.9 %collective-permute-done.52.refs_0_ = bf16[12,32,256]{2,1,0:T(8,128)(2,1)S(1)} collective-permute-done((bf16[12,32,256]{2,1,0:T(8,128)(2,1)S(1)}, bf16[12,32,256]{2,1,0:T(8,128)(2,1)S(1)}, u32[]{:S(2)}, u32[]{:S(2)}) %collective-permute-start.52) | collective-permute-done | bytes 196640 | tf_op jit(solution)/shard_map/ppermute | solution.py:28
  97.2 1.8 %shard_map.70 = f32[4,640,256]{2,1,0:T(8,128)} custom-call(s32[1,3]{1,0:T(1,128)S(1)} %bitcast.15, f32[640,256]{1,0:T(8,128)S(1)} %shard_map.66.base_ref, bf16[640,640]{1,0:T(8,128)(2,1)S(1)} %get-tuple-element.81.inv_ref, bf16[640,1536]{1,0:T(8,128)(2,1)S(1)} %get-tuple-element.74.turned_ref, ...), custom_call_target="tpu_custom_call", output_to_operand_aliasing={{}: (6, {})} | custom-call | flops 356515840 | bytes 3997696 | tf_op jit(solution)/shard_map/pallas_call | solution.py:328
  (118 shorter events, 38.2 us)
Async XLA Ops:
  2.3 10.1 %collective-permute-start = (bf16[6,32,256]{2,1,0:T(8,128)(2,1)S(1)}, bf16[6,32,256]{2,1,0:T(8,128)(2,1)S(1)}, u32[]{:S(2)}, u32[]{:S(2)}) collective-permute-start(bf16[6,32,256]{2,1,0:T(8,128)(2,1)S(1)} %get-tuple-element.49), channel_id=1, source_target_pairs={{0,2},{1,3},{2,0},{3,1},{4,6},{5,7},{6,4},{7,5},{8,10},{9,11},{10,... | collective-permute-start | bytes 294920 | tf_op jit(solution)/shard_map/ppermute | solution.py:28
  5.3 8.6 %collective-permute-start.1 = (bf16[6,32,256]{2,1,0:T(8,128)(2,1)S(1)}, bf16[6,32,256]{2,1,0:T(8,128)(2,1)S(1)}, u32[]{:S(2)}, u32[]{:S(2)}) collective-permute-start(bf16[6,32,256]{2,1,0:T(8,128)(2,1)S(1)} %get-tuple-element.50), channel_id=1, source_target_pairs={{0,4},{1,5},{2,6},{3,7},{4,0},{5,1},{6,2},{7,3},{8,12},{9,13},{10,... | collective-permute-start | bytes 294920 | tf_op jit(solution)/shard_map/ppermute | solution.py:28
  6.9 14.3 %collective-permute-start.2 = (bf16[6,32,256]{2,1,0:T(8,128)(2,1)S(1)}, bf16[6,32,256]{2,1,0:T(8,128)(2,1)S(1)}, u32[]{:S(2)}, u32[]{:S(2)}) collective-permute-start(bf16[6,32,256]{2,1,0:T(8,128)(2,1)S(1)} %get-tuple-element.51), channel_id=1, source_target_pairs={{0,6},{1,7},{2,4},{3,5},{4,2},{5,3},{6,0},{7,1},{8,14},{9,15},{10,... | collective-permute-start | bytes 294920 | tf_op jit(solution)/shard_map/ppermute | solution.py:28
  6.9 7.4 %collective-permute-start.3 = (bf16[5,32,256]{2,1,0:T(8,128)(2,1)S(1)}, bf16[5,32,256]{2,1,0:T(8,128)(2,1)S(1)}, u32[]{:S(2)}, u32[]{:S(2)}) collective-permute-start(bf16[5,32,256]{2,1,0:T(8,128)(2,1)S(1)} %get-tuple-element.46.after_ref.refs_8_), channel_id=1, source_target_pairs={{0,8},{1,9},{2,10},{3,11},{4,12},{5,13},{6,14},{7,15},{8,16},{9,17... | collective-permute-start | bytes 245768 | tf_op jit(solution)/shard_map/ppermute | solution.py:28
  8.9 9.0 %collective-permute-start.6 = (bf16[5,32,256]{2,1,0:T(8,128)(2,1)S(1)}, bf16[5,32,256]{2,1,0:T(8,128)(2,1)S(1)}, u32[]{:S(2)}, u32[]{:S(2)}) collective-permute-start(bf16[5,32,256]{2,1,0:T(8,128)(2,1)S(1)} %get-tuple-element.54), channel_id=1, source_target_pairs={{0,14},{1,15},{2,12},{3,13},{4,10},{5,11},{6,8},{7,9},{8,22},{9,23... | collective-permute-start | bytes 245768 | tf_op jit(solution)/shard_map/ppermute | solution.py:28
  12.4 7.2 %collective-permute-start.4 = (bf16[5,32,256]{2,1,0:T(8,128)(2,1)S(1)}, bf16[5,32,256]{2,1,0:T(8,128)(2,1)S(1)}, u32[]{:S(2)}, u32[]{:S(2)}) collective-permute-start(bf16[5,32,256]{2,1,0:T(8,128)(2,1)S(1)} %get-tuple-element.52), channel_id=1, source_target_pairs={{0,10},{1,11},{2,8},{3,9},{4,14},{5,15},{6,12},{7,13},{8,18},{9,19... | collective-permute-start | bytes 245768 | tf_op jit(solution)/shard_map/ppermute | solution.py:28
  14.3 7.6 %collective-permute-start.11 = (bf16[5,32,256]{2,1,0:T(8,128)(2,1)S(1)}, bf16[5,32,256]{2,1,0:T(8,128)(2,1)S(1)}, u32[]{:S(2)}, u32[]{:S(2)}) collective-permute-start(bf16[5,32,256]{2,1,0:T(8,128)(2,1)S(1)} %get-tuple-element.46.after_ref.refs_8_), channel_id=1, source_target_pairs={{0,1},{1,0},{2,3},{3,2},{4,5},{5,4},{6,7},{7,6},{8,9},{9,8},{10,11... | collective-permute-start | bytes 245768 | tf_op jit(solution)/shard_map/ppermute | solution.py:33
  24.0 7.8 %collective-permute-start.15 = (bf16[12,32,256]{2,1,0:T(8,128)(2,1)S(1)}, bf16[12,32,256]{2,1,0:T(8,128)(2,1)S(1)}, u32[]{:S(2)}, u32[]{:S(2)}) collective-permute-start(bf16[12,32,256]{2,1,0:T(8,128)(2,1)S(1)} %get-tuple-element.56), channel_id=1, source_target_pairs={{0,2},{1,3},{2,0},{3,1},{4,6},{5,7},{6,4},{7,5},{8,10},{9,11},{10,... | collective-permute-start | bytes 589832 | tf_op jit(solution)/shard_map/ppermute | solution.py:28
  25.6 10.9 %collective-permute-start.16 = (bf16[12,32,256]{2,1,0:T(8,128)(2,1)S(1)}, bf16[12,32,256]{2,1,0:T(8,128)(2,1)S(1)}, u32[]{:S(2)}, u32[]{:S(2)}) collective-permute-start(bf16[12,32,256]{2,1,0:T(8,128)(2,1)S(1)} %get-tuple-element.58), channel_id=1, source_target_pairs={{0,4},{1,5},{2,6},{3,7},{4,0},{5,1},{6,2},{7,3},{8,12},{9,13},{10,... | collective-permute-start | bytes 589832 | tf_op jit(solution)/shard_map/ppermute | solution.py:28
  26.1 10.4 %collective-permute-start.17 = (bf16[12,32,256]{2,1,0:T(8,128)(2,1)S(1)}, bf16[12,32,256]{2,1,0:T(8,128)(2,1)S(1)}, u32[]{:S(2)}, u32[]{:S(2)}) collective-permute-start(bf16[12,32,256]{2,1,0:T(8,128)(2,1)S(1)} %get-tuple-element.59), channel_id=1, source_target_pairs={{0,6},{1,7},{2,4},{3,5},{4,2},{5,3},{6,0},{7,1},{8,14},{9,15},{10,... | collective-permute-start | bytes 589832 | tf_op jit(solution)/shard_map/ppermute | solution.py:28
  37.6 7.3 %collective-permute-start.18 = (bf16[5,32,256]{2,1,0:T(8,128)(2,1)S(1)}, bf16[5,32,256]{2,1,0:T(8,128)(2,1)S(1)}, u32[]{:S(2)}, u32[]{:S(2)}) collective-permute-start(bf16[5,32,256]{2,1,0:T(8,128)(2,1)S(1)} %get-tuple-element.60.after_ref.refs_9_), channel_id=1, source_target_pairs={{0,8},{1,9},{2,10},{3,11},{4,12},{5,13},{6,14},{7,15},{8,16},{9,17... | collective-permute-start | bytes 245768 | tf_op jit(solution)/shard_map/ppermute | solution.py:28
  37.6 8.8 %collective-permute-start.19 = (bf16[5,32,256]{2,1,0:T(8,128)(2,1)S(1)}, bf16[5,32,256]{2,1,0:T(8,128)(2,1)S(1)}, u32[]{:S(2)}, u32[]{:S(2)}) collective-permute-start(bf16[5,32,256]{2,1,0:T(8,128)(2,1)S(1)} %get-tuple-element.64), channel_id=1, source_target_pairs={{0,10},{1,11},{2,8},{3,9},{4,14},{5,15},{6,12},{7,13},{8,18},{9,19... | collective-permute-start | bytes 245768 | tf_op jit(solution)/shard_map/ppermute | solution.py:28
  37.7 10.2 %collective-permute-start.20 = (bf16[5,32,256]{2,1,0:T(8,128)(2,1)S(1)}, bf16[5,32,256]{2,1,0:T(8,128)(2,1)S(1)}, u32[]{:S(2)}, u32[]{:S(2)}) collective-permute-start(bf16[5,32,256]{2,1,0:T(8,128)(2,1)S(1)} %get-tuple-element.65), channel_id=1, source_target_pairs={{0,12},{1,13},{2,14},{3,15},{4,8},{5,9},{6,10},{7,11},{8,20},{9,21... | collective-permute-start | bytes 245768 | tf_op jit(solution)/shard_map/ppermute | solution.py:28
  40.1 9.1 %collective-permute-start.21 = (bf16[5,32,256]{2,1,0:T(8,128)(2,1)S(1)}, bf16[5,32,256]{2,1,0:T(8,128)(2,1)S(1)}, u32[]{:S(2)}, u32[]{:S(2)}) collective-permute-start(bf16[5,32,256]{2,1,0:T(8,128)(2,1)S(1)} %get-tuple-element.66), channel_id=1, source_target_pairs={{0,14},{1,15},{2,12},{3,13},{4,10},{5,11},{6,8},{7,9},{8,22},{9,23... | collective-permute-start | bytes 245768 | tf_op jit(solution)/shard_map/ppermute | solution.py:28
  54.1 7.8 %collective-permute-start.33 = (bf16[12,32,256]{2,1,0:T(8,128)(2,1)S(1)}, bf16[12,32,256]{2,1,0:T(8,128)(2,1)S(1)}, u32[]{:S(2)}, u32[]{:S(2)}) collective-permute-start(bf16[12,32,256]{2,1,0:T(8,128)(2,1)S(1)} %get-tuple-element.68), channel_id=1, source_target_pairs={{0,2},{1,3},{2,0},{3,1},{4,6},{5,7},{6,4},{7,5},{8,10},{9,11},{10,... | collective-permute-start | bytes 589832 | tf_op jit(solution)/shard_map/ppermute | solution.py:28
  55.6 11.1 %collective-permute-start.34 = (bf16[12,32,256]{2,1,0:T(8,128)(2,1)S(1)}, bf16[12,32,256]{2,1,0:T(8,128)(2,1)S(1)}, u32[]{:S(2)}, u32[]{:S(2)}) collective-permute-start(bf16[12,32,256]{2,1,0:T(8,128)(2,1)S(1)} %get-tuple-element.70), channel_id=1, source_target_pairs={{0,4},{1,5},{2,6},{3,7},{4,0},{5,1},{6,2},{7,3},{8,12},{9,13},{10,... | collective-permute-start | bytes 589832 | tf_op jit(solution)/shard_map/ppermute | solution.py:28
  56.2 10.4 %collective-permute-start.35 = (bf16[12,32,256]{2,1,0:T(8,128)(2,1)S(1)}, bf16[12,32,256]{2,1,0:T(8,128)(2,1)S(1)}, u32[]{:S(2)}, u32[]{:S(2)}) collective-permute-start(bf16[12,32,256]{2,1,0:T(8,128)(2,1)S(1)} %get-tuple-element.71), channel_id=1, source_target_pairs={{0,6},{1,7},{2,4},{3,5},{4,2},{5,3},{6,0},{7,1},{8,14},{9,15},{10,... | collective-permute-start | bytes 589832 | tf_op jit(solution)/shard_map/ppermute | solution.py:28
  67.8 7.5 %collective-permute-start.36 = (bf16[5,32,256]{2,1,0:T(8,128)(2,1)S(1)}, bf16[5,32,256]{2,1,0:T(8,128)(2,1)S(1)}, u32[]{:S(2)}, u32[]{:S(2)}) collective-permute-start(bf16[5,32,256]{2,1,0:T(8,128)(2,1)S(1)} %get-tuple-element.72.after_ref.refs_10_), channel_id=1, source_target_pairs={{0,8},{1,9},{2,10},{3,11},{4,12},{5,13},{6,14},{7,15},{8,16},{9,17... | collective-permute-start | bytes 245768 | tf_op jit(solution)/shard_map/ppermute | solution.py:28
  67.8 9.0 %collective-permute-start.37 = (bf16[5,32,256]{2,1,0:T(8,128)(2,1)S(1)}, bf16[5,32,256]{2,1,0:T(8,128)(2,1)S(1)}, u32[]{:S(2)}, u32[]{:S(2)}) collective-permute-start(bf16[5,32,256]{2,1,0:T(8,128)(2,1)S(1)} %get-tuple-element.76), channel_id=1, source_target_pairs={{0,10},{1,11},{2,8},{3,9},{4,14},{5,15},{6,12},{7,13},{8,18},{9,19... | collective-permute-start | bytes 245768 | tf_op jit(solution)/shard_map/ppermute | solution.py:28
  68.2 10.1 %collective-permute-start.38 = (bf16[5,32,256]{2,1,0:T(8,128)(2,1)S(1)}, bf16[5,32,256]{2,1,0:T(8,128)(2,1)S(1)}, u32[]{:S(2)}, u32[]{:S(2)}) collective-permute-start(bf16[5,32,256]{2,1,0:T(8,128)(2,1)S(1)} %get-tuple-element.77), channel_id=1, source_target_pairs={{0,12},{1,13},{2,14},{3,15},{4,8},{5,9},{6,10},{7,11},{8,20},{9,21... | collective-permute-start | bytes 245768 | tf_op jit(solution)/shard_map/ppermute | solution.py:28
  69.9 9.7 %collective-permute-start.39 = (bf16[5,32,256]{2,1,0:T(8,128)(2,1)S(1)}, bf16[5,32,256]{2,1,0:T(8,128)(2,1)S(1)}, u32[]{:S(2)}, u32[]{:S(2)}) collective-permute-start(bf16[5,32,256]{2,1,0:T(8,128)(2,1)S(1)} %get-tuple-element.78), channel_id=1, source_target_pairs={{0,14},{1,15},{2,12},{3,13},{4,10},{5,11},{6,8},{7,9},{8,22},{9,23... | collective-permute-start | bytes 245768 | tf_op jit(solution)/shard_map/ppermute | solution.py:28
  84.7 8.0 %collective-permute-start.51 = (bf16[12,32,256]{2,1,0:T(8,128)(2,1)S(1)}, bf16[12,32,256]{2,1,0:T(8,128)(2,1)S(1)}, u32[]{:S(2)}, u32[]{:S(2)}) collective-permute-start(bf16[12,32,256]{2,1,0:T(8,128)(2,1)S(1)} %get-tuple-element.80), channel_id=1, source_target_pairs={{0,2},{1,3},{2,0},{3,1},{4,6},{5,7},{6,4},{7,5},{8,10},{9,11},{10,... | collective-permute-start | bytes 589832 | tf_op jit(solution)/shard_map/ppermute | solution.py:28
  86.1 11.1 %collective-permute-start.52 = (bf16[12,32,256]{2,1,0:T(8,128)(2,1)S(1)}, bf16[12,32,256]{2,1,0:T(8,128)(2,1)S(1)}, u32[]{:S(2)}, u32[]{:S(2)}) collective-permute-start(bf16[12,32,256]{2,1,0:T(8,128)(2,1)S(1)} %get-tuple-element.82), channel_id=1, source_target_pairs={{0,4},{1,5},{2,6},{3,7},{4,0},{5,1},{6,2},{7,3},{8,12},{9,13},{10,... | collective-permute-start | bytes 589832 | tf_op jit(solution)/shard_map/ppermute | solution.py:28
  86.8 10.4 %collective-permute-start.53 = (bf16[12,32,256]{2,1,0:T(8,128)(2,1)S(1)}, bf16[12,32,256]{2,1,0:T(8,128)(2,1)S(1)}, u32[]{:S(2)}, u32[]{:S(2)}) collective-permute-start(bf16[12,32,256]{2,1,0:T(8,128)(2,1)S(1)} %get-tuple-element.83), channel_id=1, source_target_pairs={{0,6},{1,7},{2,4},{3,5},{4,2},{5,3},{6,0},{7,1},{8,14},{9,15},{10,... | collective-permute-start | bytes 589832 | tf_op jit(solution)/shard_map/ppermute | solution.py:28
  (32 other events, 93.6 us)

commit v2 on v1

--- a/solution.py
+++ b/solution.py
@@ -76,22 +76,23 @@
             piece_ref[i] = x_ref[pl.ds(start, quarter), :].astype(jnp.bfloat16)
 
 
-def first_kernel(tile, list_ref, rhs_hbm, inv_hbm, x_ref, *refs):
-    piece_refs, noted_refs = refs[:CHIPS], refs[CHIPS:-4]
-    rhs_ref, inv_ref, note_ref, sems = refs[-4:]
+def first_kernel(tile, list_hbm, rhs_hbm, inv_hbm, x_ref, *refs):
+    piece_refs, noted_refs = refs[:CHIPS], refs[CHIPS:-5]
+    rhs_ref, inv_ref, list_ref, note_ref, sems = refs[-5:]
     copies = [
         pltpu.make_async_copy(rhs_hbm.at[0], rhs_ref, sems.at[0]),
         pltpu.make_async_copy(inv_hbm.at[0], inv_ref, sems.at[1]),
+        pltpu.make_async_copy(list_hbm, list_ref, sems.at[2]),
     ]
     for copy in copies:
         copy.start()
+    for copy in copies:
+        copy.wait()
     levels, _, slots = list_ref.shape
     note_ref[...] = jnp.zeros_like(note_ref)
     for level in range(levels):
         note_ref[level : level + 1, :slots] = list_ref[level].astype(jnp.float32)
     note = note_ref[...].astype(jnp.bfloat16)
-    for copy in copies:
-        copy.wait()
     solve_rows(inv_ref, rhs_ref, x_ref, piece_refs, tile)
     for piece_ref, noted_ref in zip(piece_refs[1:], noted_refs):
         per_node = piece_ref.shape[0]
@@ -222,9 +223,14 @@
     part_moved = 2 * slots * quarter * (width + columns) + 8 * width * columns
     semaphores = pltpu.SemaphoreType.DMA
 
-    rhs, inv_diag, factor = (
+    rhs, inv_diag, factor, tile_list = (
         pltpu.with_memory_space_constraint(value, pltpu.HBM)
-        for value in (rhs, inv_diag, factor.reshape(-1, slots, CHIPS, quarter, width))
+        for value in (
+            rhs,
+            inv_diag,
+            factor.reshape(-1, slots, CHIPS, quarter, width),
+            tile_list,
+        )
     )
 
     assert (levels - 1) * pool <= 256 and levels - 1 <= quarter and slots <= columns
@@ -233,15 +239,16 @@
     solution, *outputs = call(
         functools.partial(first_kernel, tile),
         shapes + (noted,) * (CHIPS - 1),
-        [VMEM, HBM, HBM],
+        [HBM] * 3,
         [VMEM] * (len(shapes) + CHIPS - 1),
         solve_flops,
         2 * width * (width + 4 * columns),
         [
             pltpu.VMEM((width, columns), half),
             pltpu.VMEM((width, width), half),
+            pltpu.VMEM(tile_list.shape, jnp.int32),
             pltpu.VMEM((quarter, columns), jnp.float32),
-            semaphores((2,)),
+            semaphores((3,)),
         ],
     )(tile_list, rhs, inv_diag)
     pieces, noted = outputs[:CHIPS], outputs[CHIPS:]
@@ -288,7 +295,12 @@
             [semaphores],
             {} if level == 1 else {1: 0},
         )(*((solution,) if level == 1 else (solution, out)))
-        fresh = previous + [swap(value) for value in previous] + own + [swap(value) for value in own]
+        fresh = (
+            previous
+            + [swap(value) for value in previous]
+            + own
+            + [swap(value) for value in own]
+        )
 
         inputs = pools + fresh
         packed = jax.ShapeDtypeStruct((pool, quarter, columns), half)

time: 99.2 us -> 98.5 us (level)
  no operation moved by 1% of the time
where the time goes in v2:
time: 98.5 us; the launch traced here: 98.3 us
  starting transfers between devices  46.1 us (47%)
  waiting for transfers between devices  35.2 us (36%)
  Pallas kernels  16.4 us (17%)
    ppermute x30, starting transfers between devices, send(): return lax.ppermute(value, 'nodes', route)  42.8 us
    ppermute x30, waiting for transfers between devices, send(): return lax.ppermute(value, 'nodes', route)  32.1 us
    pallas_call x3, Pallas kernels, body(): call(functools.partial(load_kernel, level), (jax.ShapeDtypeStruct((width,...  5.7 us
    ppermute x24, starting transfers between devices, swap(): return lax.ppermute(value, 'nodes', [(i, i ^ 1) for i in range(size)])  3.29 us
    ppermute x24, waiting for transfers between devices, swap(): return lax.ppermute(value, 'nodes', [(i, i ^ 1) for i in range(size)])  3.02 us
    pallas_call x3, Pallas kernels, body(): call(functools.partial(store_kernel, level - 1), out_shape, [VMEM] if lev...  2.54 us
    pallas_call x2, Pallas kernels, body(): level_call(out_shape=shapes, in_specs=in_specs, out_specs=[VMEM] * len(sh...  2.19 us
  transfers between devices with their start and end apart: 54, of which 29 were waited for; matrix products, arithmetic and copies ran while one was open for 0% of the time, Pallas kernels for 10%

profile of v2, /device:TPU:0, one launch (start us, length us, event | category | flops | bytes accessed | tf_op | source)
XLA Modules:
  0.0 98.3 jit_solution(2301846990829513669)
XLA Ops:
  0.0 1.6 %shard_map.55 = (f32[640,256]{1,0:T(8,128)S(1)}, bf16[5,32,256]{2,1,0:T(8,128)(2,1)S(1)}, bf16[5,32,256]{2,1,0:T(8,128)(2,1)S(1)}, bf16[5,32,256]{2,1,0:T(8,128)...) custom-call(s32[3,1,12]{2,1,0:T(1,128)} %list_hbm.1, ...), custom_call_target="tpu_custom_call" | custom-call | flops 104857600 | bytes 2129920 | tf_op jit(solution)/shard_map/pallas_call | solution.py:239
  1.6 3.0 %collective-permute-start = (bf16[6,32,256]{2,1,0:T(8,128)(2,1)S(1)}, bf16[6,32,256]{2,1,0:T(8,128)(2,1)S(1)}, u32[]{:S(2)}, u32[]{:S(2)}) collective-permute-start(bf16[6,32,256]{2,1,0:T(8,128)(2,1)S(1)} %get-tuple-element.49), channel_id=1, source_target_pairs={{0,2},{1,3},{2,0},{3,1},{4,6},{5,7},{6,4},{7,5},{8,10},{9,11},{10,... | collective-permute-start | bytes 294920 | tf_op jit(solution)/shard_map/ppermute | solution.py:28
  4.7 1.5 %collective-permute-start.1 = (bf16[6,32,256]{2,1,0:T(8,128)(2,1)S(1)}, bf16[6,32,256]{2,1,0:T(8,128)(2,1)S(1)}, u32[]{:S(2)}, u32[]{:S(2)}) collective-permute-start(bf16[6,32,256]{2,1,0:T(8,128)(2,1)S(1)} %get-tuple-element.50), channel_id=1, source_target_pairs={{0,4},{1,5},{2,6},{3,7},{4,0},{5,1},{6,2},{7,3},{8,12},{9,13},{10,... | collective-permute-start | bytes 294920 | tf_op jit(solution)/shard_map/ppermute | solution.py:28
  6.2 2.0 %collective-permute-start.3 = (bf16[5,32,256]{2,1,0:T(8,128)(2,1)S(1)}, bf16[5,32,256]{2,1,0:T(8,128)(2,1)S(1)}, u32[]{:S(2)}, u32[]{:S(2)}) collective-permute-start(bf16[5,32,256]{2,1,0:T(8,128)(2,1)S(1)} %get-tuple-element.46.after_ref.refs_8_), channel_id=1, source_target_pairs={{0,8},{1,9},{2,10},{3,11},{4,12},{5,13},{6,14},{7,15},{8,16},{9,17... | collective-permute-start | bytes 245768 | tf_op jit(solution)/shard_map/ppermute | solution.py:28
  8.2 3.5 %collective-permute-start.6 = (bf16[5,32,256]{2,1,0:T(8,128)(2,1)S(1)}, bf16[5,32,256]{2,1,0:T(8,128)(2,1)S(1)}, u32[]{:S(2)}, u32[]{:S(2)}) collective-permute-start(bf16[5,32,256]{2,1,0:T(8,128)(2,1)S(1)} %get-tuple-element.54), channel_id=1, source_target_pairs={{0,14},{1,15},{2,12},{3,13},{4,10},{5,11},{6,8},{7,9},{8,22},{9,23... | collective-permute-start | bytes 245768 | tf_op jit(solution)/shard_map/ppermute | solution.py:28
  11.7 1.6 %collective-permute-start.4 = (bf16[5,32,256]{2,1,0:T(8,128)(2,1)S(1)}, bf16[5,32,256]{2,1,0:T(8,128)(2,1)S(1)}, u32[]{:S(2)}, u32[]{:S(2)}) collective-permute-start(bf16[5,32,256]{2,1,0:T(8,128)(2,1)S(1)} %get-tuple-element.52), channel_id=1, source_target_pairs={{0,10},{1,11},{2,8},{3,9},{4,14},{5,15},{6,12},{7,13},{8,18},{9,19... | collective-permute-start | bytes 245768 | tf_op jit(solution)/shard_map/ppermute | solution.py:28
  13.7 3.5 %collective-permute-done.6.refs_3_ = bf16[5,32,256]{2,1,0:T(8,128)(2,1)S(1)} collective-permute-done((bf16[5,32,256]{2,1,0:T(8,128)(2,1)S(1)}, bf16[5,32,256]{2,1,0:T(8,128)(2,1)S(1)}, u32[]{:S(2)}, u32[]{:S(2)}) %collective-permute-start.6) | collective-permute-done | bytes 81952 | tf_op jit(solution)/shard_map/ppermute | solution.py:28
  17.3 1.7 %collective-permute-done.4.refs_1_ = bf16[5,32,256]{2,1,0:T(8,128)(2,1)S(1)} collective-permute-done((bf16[5,32,256]{2,1,0:T(8,128)(2,1)S(1)}, bf16[5,32,256]{2,1,0:T(8,128)(2,1)S(1)}, u32[]{:S(2)}, u32[]{:S(2)}) %collective-permute-start.4) | collective-permute-done | bytes 81952 | tf_op jit(solution)/shard_map/ppermute | solution.py:28
  19.0 1.5 %collective-permute-done.5.refs_2_ = bf16[5,32,256]{2,1,0:T(8,128)(2,1)S(1)} collective-permute-done((bf16[5,32,256]{2,1,0:T(8,128)(2,1)S(1)}, bf16[5,32,256]{2,1,0:T(8,128)(2,1)S(1)}, u32[]{:S(2)}, u32[]{:S(2)}) %collective-permute-start.5) | collective-permute-done | bytes 81952 | tf_op jit(solution)/shard_map/ppermute | solution.py:28
  23.3 1.6 %collective-permute-start.15 = (bf16[12,32,256]{2,1,0:T(8,128)(2,1)S(1)}, bf16[12,32,256]{2,1,0:T(8,128)(2,1)S(1)}, u32[]{:S(2)}, u32[]{:S(2)}) collective-permute-start(bf16[12,32,256]{2,1,0:T(8,128)(2,1)S(1)} %get-tuple-element.56), channel_id=1, source_target_pairs={{0,2},{1,3},{2,0},{3,1},{4,6},{5,7},{6,4},{7,5},{8,10},{9,11},{10,... | collective-permute-start | bytes 589832 | tf_op jit(solution)/shard_map/ppermute | solution.py:28
  25.4 1.5 %collective-permute-start.17 = (bf16[12,32,256]{2,1,0:T(8,128)(2,1)S(1)}, bf16[12,32,256]{2,1,0:T(8,128)(2,1)S(1)}, u32[]{:S(2)}, u32[]{:S(2)}) collective-permute-start(bf16[12,32,256]{2,1,0:T(8,128)(2,1)S(1)} %get-tuple-element.59), channel_id=1, source_target_pairs={{0,6},{1,7},{2,4},{3,5},{4,2},{5,3},{6,0},{7,1},{8,14},{9,15},{10,... | collective-permute-start | bytes 589832 | tf_op jit(solution)/shard_map/ppermute | solution.py:28
  26.9 1.9 %shard_map.56 = (bf16[640,256]{1,0:T(8,128)(2,1)S(1)}, bf16[640,640]{1,0:T(8,128)(2,1)S(1)}, bf16[640,1536]{1,0:T(8,128)(2,1)S(1)}) custom-call(bf16[5,32,256]{2,1,0:T(8,128)(2,1)S(1)} %get-tuple-element.46.after_ref.refs_8_, bf16[4,640,256]{2,1,0:T(8,128)(2,1)} %rhs_hbm.7, bf16[4,640,640]{2,1,0:T(8,128)(2,1)} %inv_hbm.7, bf16[3,12,4,32,640]{4,3,2,1,0:T(8,128)(2,1)} %bitcast.16), custom_call_target="tpu_custom_call" | custom-call | bytes 3112960 | tf_op jit(solution)/shard_map/pallas_call | solution.py:275
  28.8 2.4 %collective-permute-done.15.refs_1_ = bf16[12,32,256]{2,1,0:T(8,128)(2,1)S(1)} collective-permute-done((bf16[12,32,256]{2,1,0:T(8,128)(2,1)S(1)}, bf16[12,32,256]{2,1,0:T(8,128)(2,1)S(1)}, u32[]{:S(2)}, u32[]{:S(2)}) %collective-permute-start.15) | collective-permute-done | bytes 196640 | tf_op jit(solution)/shard_map/ppermute | solution.py:28
  31.7 4.1 %collective-permute-done.16.refs_0_ = bf16[12,32,256]{2,1,0:T(8,128)(2,1)S(1)} collective-permute-done((bf16[12,32,256]{2,1,0:T(8,128)(2,1)S(1)}, bf16[12,32,256]{2,1,0:T(8,128)(2,1)S(1)}, u32[]{:S(2)}, u32[]{:S(2)}) %collective-permute-start.16) | collective-permute-done | bytes 196640 | tf_op jit(solution)/shard_map/ppermute | solution.py:28
  37.0 2.4 %collective-permute-start.20 = (bf16[5,32,256]{2,1,0:T(8,128)(2,1)S(1)}, bf16[5,32,256]{2,1,0:T(8,128)(2,1)S(1)}, u32[]{:S(2)}, u32[]{:S(2)}) collective-permute-start(bf16[5,32,256]{2,1,0:T(8,128)(2,1)S(1)} %get-tuple-element.65), channel_id=1, source_target_pairs={{0,12},{1,13},{2,14},{3,15},{4,8},{5,9},{6,10},{7,11},{8,20},{9,21... | collective-permute-start | bytes 245768 | tf_op jit(solution)/shard_map/ppermute | solution.py:28
  39.5 4.2 %collective-permute-start.21 = (bf16[5,32,256]{2,1,0:T(8,128)(2,1)S(1)}, bf16[5,32,256]{2,1,0:T(8,128)(2,1)S(1)}, u32[]{:S(2)}, u32[]{:S(2)}) collective-permute-start(bf16[5,32,256]{2,1,0:T(8,128)(2,1)S(1)} %get-tuple-element.66), channel_id=1, source_target_pairs={{0,14},{1,15},{2,12},{3,13},{4,10},{5,11},{6,8},{7,9},{8,22},{9,23... | collective-permute-start | bytes 245768 | tf_op jit(solution)/shard_map/ppermute | solution.py:28
  57.0 1.9 %shard_map.60 = (bf16[640,256]{1,0:T(8,128)(2,1)S(1)}, bf16[640,640]{1,0:T(8,128)(2,1)S(1)}, bf16[640,1536]{1,0:T(8,128)(2,1)S(1)}) custom-call(bf16[5,32,256]{2,1,0:T(8,128)(2,1)S(1)} %get-tuple-element.60.after_ref.refs_9_, bf16[4,640,256]{2,1,0:T(8,128)(2,1)} %rhs_hbm.7, bf16[4,640,640]{2,1,0:T(8,128)(2,1)} %inv_hbm.7, bf16[3,12,4,32,640]{4,3,2,1,0:T(8,128)(2,1)} %bitcast.17), custom_call_target="tpu_custom_call" | custom-call | bytes 3112960 | tf_op jit(solution)/shard_map/pallas_call | solution.py:275
  58.9 2.4 %collective-permute-done.33.refs_1_ = bf16[12,32,256]{2,1,0:T(8,128)(2,1)S(1)} collective-permute-done((bf16[12,32,256]{2,1,0:T(8,128)(2,1)S(1)}, bf16[12,32,256]{2,1,0:T(8,128)(2,1)S(1)}, u32[]{:S(2)}, u32[]{:S(2)}) %collective-permute-start.33) | collective-permute-done | bytes 196640 | tf_op jit(solution)/shard_map/ppermute | solution.py:28
  61.8 4.2 %collective-permute-done.34.refs_0_ = bf16[12,32,256]{2,1,0:T(8,128)(2,1)S(1)} collective-permute-done((bf16[12,32,256]{2,1,0:T(8,128)(2,1)S(1)}, bf16[12,32,256]{2,1,0:T(8,128)(2,1)S(1)}, u32[]{:S(2)}, u32[]{:S(2)}) %collective-permute-start.34) | collective-permute-done | bytes 196640 | tf_op jit(solution)/shard_map/ppermute | solution.py:28
  67.6 1.7 %collective-permute-start.38 = (bf16[5,32,256]{2,1,0:T(8,128)(2,1)S(1)}, bf16[5,32,256]{2,1,0:T(8,128)(2,1)S(1)}, u32[]{:S(2)}, u32[]{:S(2)}) collective-permute-start(bf16[5,32,256]{2,1,0:T(8,128)(2,1)S(1)} %get-tuple-element.77), channel_id=1, source_target_pairs={{0,12},{1,13},{2,14},{3,15},{4,8},{5,9},{6,10},{7,11},{8,20},{9,21... | collective-permute-start | bytes 245768 | tf_op jit(solution)/shard_map/ppermute | solution.py:28
  69.3 4.6 %collective-permute-start.39 = (bf16[5,32,256]{2,1,0:T(8,128)(2,1)S(1)}, bf16[5,32,256]{2,1,0:T(8,128)(2,1)S(1)}, u32[]{:S(2)}, u32[]{:S(2)}) collective-permute-start(bf16[5,32,256]{2,1,0:T(8,128)(2,1)S(1)} %get-tuple-element.78), channel_id=1, source_target_pairs={{0,14},{1,15},{2,12},{3,13},{4,10},{5,11},{6,8},{7,9},{8,22},{9,23... | collective-permute-start | bytes 245768 | tf_op jit(solution)/shard_map/ppermute | solution.py:28
  89.2 1.9 %shard_map.64 = (bf16[640,256]{1,0:T(8,128)(2,1)S(1)}, bf16[640,640]{1,0:T(8,128)(2,1)S(1)}, bf16[640,1536]{1,0:T(8,128)(2,1)S(1)}) custom-call(bf16[5,32,256]{2,1,0:T(8,128)(2,1)S(1)} %get-tuple-element.72.after_ref.refs_10_, bf16[4,640,256]{2,1,0:T(8,128)(2,1)} %rhs_hbm.7, bf16[4,640,640]{2,1,0:T(8,128)(2,1)} %inv_hbm.7, bf16[3,12,4,32,640]{4,3,2,1,0:T(8,128)(2,1)} %bitcast.18), custom_call_target="tpu_custom_call" | custom-call | bytes 3112960 | tf_op jit(solution)/shard_map/pallas_call | solution.py:275
  92.5 3.9 %collective-permute-done.52.refs_0_ = bf16[12,32,256]{2,1,0:T(8,128)(2,1)S(1)} collective-permute-done((bf16[12,32,256]{2,1,0:T(8,128)(2,1)S(1)}, bf16[12,32,256]{2,1,0:T(8,128)(2,1)S(1)}, u32[]{:S(2)}, u32[]{:S(2)}) %collective-permute-start.52) | collective-permute-done | bytes 196640 | tf_op jit(solution)/shard_map/ppermute | solution.py:28
  96.5 1.8 %shard_map.70 = f32[4,640,256]{2,1,0:T(8,128)} custom-call(s32[1,3]{1,0:T(1,128)S(1)} %bitcast.15, f32[640,256]{1,0:T(8,128)S(1)} %shard_map.66.base_ref, bf16[640,640]{1,0:T(8,128)(2,1)S(1)} %get-tuple-element.81.inv_ref, bf16[640,1536]{1,0:T(8,128)(2,1)S(1)} %get-tuple-element.74.turned_ref, ...), custom_call_target="tpu_custom_call", output_to_operand_aliasing={{}: (6, {})} | custom-call | flops 356515840 | bytes 3997696 | tf_op jit(solution)/shard_map/pallas_call | solution.py:340
  (116 shorter events, 37.5 us)
Async XLA Ops:
  1.6 10.1 %collective-permute-start = (bf16[6,32,256]{2,1,0:T(8,128)(2,1)S(1)}, bf16[6,32,256]{2,1,0:T(8,128)(2,1)S(1)}, u32[]{:S(2)}, u32[]{:S(2)}) collective-permute-start(bf16[6,32,256]{2,1,0:T(8,128)(2,1)S(1)} %get-tuple-element.49), channel_id=1, source_target_pairs={{0,2},{1,3},{2,0},{3,1},{4,6},{5,7},{6,4},{7,5},{8,10},{9,11},{10,... | collective-permute-start | bytes 294920 | tf_op jit(solution)/shard_map/ppermute | solution.py:28
  4.7 8.7 %collective-permute-start.1 = (bf16[6,32,256]{2,1,0:T(8,128)(2,1)S(1)}, bf16[6,32,256]{2,1,0:T(8,128)(2,1)S(1)}, u32[]{:S(2)}, u32[]{:S(2)}) collective-permute-start(bf16[6,32,256]{2,1,0:T(8,128)(2,1)S(1)} %get-tuple-element.50), channel_id=1, source_target_pairs={{0,4},{1,5},{2,6},{3,7},{4,0},{5,1},{6,2},{7,3},{8,12},{9,13},{10,... | collective-permute-start | bytes 294920 | tf_op jit(solution)/shard_map/ppermute | solution.py:28
  6.2 14.3 %collective-permute-start.2 = (bf16[6,32,256]{2,1,0:T(8,128)(2,1)S(1)}, bf16[6,32,256]{2,1,0:T(8,128)(2,1)S(1)}, u32[]{:S(2)}, u32[]{:S(2)}) collective-permute-start(bf16[6,32,256]{2,1,0:T(8,128)(2,1)S(1)} %get-tuple-element.51), channel_id=1, source_target_pairs={{0,6},{1,7},{2,4},{3,5},{4,2},{5,3},{6,0},{7,1},{8,14},{9,15},{10,... | collective-permute-start | bytes 294920 | tf_op jit(solution)/shard_map/ppermute | solution.py:28
  6.2 7.4 %collective-permute-start.3 = (bf16[5,32,256]{2,1,0:T(8,128)(2,1)S(1)}, bf16[5,32,256]{2,1,0:T(8,128)(2,1)S(1)}, u32[]{:S(2)}, u32[]{:S(2)}) collective-permute-start(bf16[5,32,256]{2,1,0:T(8,128)(2,1)S(1)} %get-tuple-element.46.after_ref.refs_8_), channel_id=1, source_target_pairs={{0,8},{1,9},{2,10},{3,11},{4,12},{5,13},{6,14},{7,15},{8,16},{9,17... | collective-permute-start | bytes 245768 | tf_op jit(solution)/shard_map/ppermute | solution.py:28
  8.2 9.0 %collective-permute-start.6 = (bf16[5,32,256]{2,1,0:T(8,128)(2,1)S(1)}, bf16[5,32,256]{2,1,0:T(8,128)(2,1)S(1)}, u32[]{:S(2)}, u32[]{:S(2)}) collective-permute-start(bf16[5,32,256]{2,1,0:T(8,128)(2,1)S(1)} %get-tuple-element.54), channel_id=1, source_target_pairs={{0,14},{1,15},{2,12},{3,13},{4,10},{5,11},{6,8},{7,9},{8,22},{9,23... | collective-permute-start | bytes 245768 | tf_op jit(solution)/shard_map/ppermute | solution.py:28
  11.7 7.2 %collective-permute-start.4 = (bf16[5,32,256]{2,1,0:T(8,128)(2,1)S(1)}, bf16[5,32,256]{2,1,0:T(8,128)(2,1)S(1)}, u32[]{:S(2)}, u32[]{:S(2)}) collective-permute-start(bf16[5,32,256]{2,1,0:T(8,128)(2,1)S(1)} %get-tuple-element.52), channel_id=1, source_target_pairs={{0,10},{1,11},{2,8},{3,9},{4,14},{5,15},{6,12},{7,13},{8,18},{9,19... | collective-permute-start | bytes 245768 | tf_op jit(solution)/shard_map/ppermute | solution.py:28
  13.7 7.6 %collective-permute-start.11 = (bf16[5,32,256]{2,1,0:T(8,128)(2,1)S(1)}, bf16[5,32,256]{2,1,0:T(8,128)(2,1)S(1)}, u32[]{:S(2)}, u32[]{:S(2)}) collective-permute-start(bf16[5,32,256]{2,1,0:T(8,128)(2,1)S(1)} %get-tuple-element.46.after_ref.refs_8_), channel_id=1, source_target_pairs={{0,1},{1,0},{2,3},{3,2},{4,5},{5,4},{6,7},{7,6},{8,9},{9,8},{10,11... | collective-permute-start | bytes 245768 | tf_op jit(solution)/shard_map/ppermute | solution.py:33
  23.3 7.8 %collective-permute-start.15 = (bf16[12,32,256]{2,1,0:T(8,128)(2,1)S(1)}, bf16[12,32,256]{2,1,0:T(8,128)(2,1)S(1)}, u32[]{:S(2)}, u32[]{:S(2)}) collective-permute-start(bf16[12,32,256]{2,1,0:T(8,128)(2,1)S(1)} %get-tuple-element.56), channel_id=1, source_target_pairs={{0,2},{1,3},{2,0},{3,1},{4,6},{5,7},{6,4},{7,5},{8,10},{9,11},{10,... | collective-permute-start | bytes 589832 | tf_op jit(solution)/shard_map/ppermute | solution.py:28
  24.9 10.9 %collective-permute-start.16 = (bf16[12,32,256]{2,1,0:T(8,128)(2,1)S(1)}, bf16[12,32,256]{2,1,0:T(8,128)(2,1)S(1)}, u32[]{:S(2)}, u32[]{:S(2)}) collective-permute-start(bf16[12,32,256]{2,1,0:T(8,128)(2,1)S(1)} %get-tuple-element.58), channel_id=1, source_target_pairs={{0,4},{1,5},{2,6},{3,7},{4,0},{5,1},{6,2},{7,3},{8,12},{9,13},{10,... | collective-permute-start | bytes 589832 | tf_op jit(solution)/shard_map/ppermute | solution.py:28
  25.4 10.4 %collective-permute-start.17 = (bf16[12,32,256]{2,1,0:T(8,128)(2,1)S(1)}, bf16[12,32,256]{2,1,0:T(8,128)(2,1)S(1)}, u32[]{:S(2)}, u32[]{:S(2)}) collective-permute-start(bf16[12,32,256]{2,1,0:T(8,128)(2,1)S(1)} %get-tuple-element.59), channel_id=1, source_target_pairs={{0,6},{1,7},{2,4},{3,5},{4,2},{5,3},{6,0},{7,1},{8,14},{9,15},{10,... | collective-permute-start | bytes 589832 | tf_op jit(solution)/shard_map/ppermute | solution.py:28
  36.9 7.3 %collective-permute-start.18 = (bf16[5,32,256]{2,1,0:T(8,128)(2,1)S(1)}, bf16[5,32,256]{2,1,0:T(8,128)(2,1)S(1)}, u32[]{:S(2)}, u32[]{:S(2)}) collective-permute-start(bf16[5,32,256]{2,1,0:T(8,128)(2,1)S(1)} %get-tuple-element.60.after_ref.refs_9_), channel_id=1, source_target_pairs={{0,8},{1,9},{2,10},{3,11},{4,12},{5,13},{6,14},{7,15},{8,16},{9,17... | collective-permute-start | bytes 245768 | tf_op jit(solution)/shard_map/ppermute | solution.py:28
  37.0 8.8 %collective-permute-start.19 = (bf16[5,32,256]{2,1,0:T(8,128)(2,1)S(1)}, bf16[5,32,256]{2,1,0:T(8,128)(2,1)S(1)}, u32[]{:S(2)}, u32[]{:S(2)}) collective-permute-start(bf16[5,32,256]{2,1,0:T(8,128)(2,1)S(1)} %get-tuple-element.64), channel_id=1, source_target_pairs={{0,10},{1,11},{2,8},{3,9},{4,14},{5,15},{6,12},{7,13},{8,18},{9,19... | collective-permute-start | bytes 245768 | tf_op jit(solution)/shard_map/ppermute | solution.py:28
  37.0 10.2 %collective-permute-start.20 = (bf16[5,32,256]{2,1,0:T(8,128)(2,1)S(1)}, bf16[5,32,256]{2,1,0:T(8,128)(2,1)S(1)}, u32[]{:S(2)}, u32[]{:S(2)}) collective-permute-start(bf16[5,32,256]{2,1,0:T(8,128)(2,1)S(1)} %get-tuple-element.65), channel_id=1, source_target_pairs={{0,12},{1,13},{2,14},{3,15},{4,8},{5,9},{6,10},{7,11},{8,20},{9,21... | collective-permute-start | bytes 245768 | tf_op jit(solution)/shard_map/ppermute | solution.py:28
  39.5 9.1 %collective-permute-start.21 = (bf16[5,32,256]{2,1,0:T(8,128)(2,1)S(1)}, bf16[5,32,256]{2,1,0:T(8,128)(2,1)S(1)}, u32[]{:S(2)}, u32[]{:S(2)}) collective-permute-start(bf16[5,32,256]{2,1,0:T(8,128)(2,1)S(1)} %get-tuple-element.66), channel_id=1, source_target_pairs={{0,14},{1,15},{2,12},{3,13},{4,10},{5,11},{6,8},{7,9},{8,22},{9,23... | collective-permute-start | bytes 245768 | tf_op jit(solution)/shard_map/ppermute | solution.py:28
  53.4 7.8 %collective-permute-start.33 = (bf16[12,32,256]{2,1,0:T(8,128)(2,1)S(1)}, bf16[12,32,256]{2,1,0:T(8,128)(2,1)S(1)}, u32[]{:S(2)}, u32[]{:S(2)}) collective-permute-start(bf16[12,32,256]{2,1,0:T(8,128)(2,1)S(1)} %get-tuple-element.68), channel_id=1, source_target_pairs={{0,2},{1,3},{2,0},{3,1},{4,6},{5,7},{6,4},{7,5},{8,10},{9,11},{10,... | collective-permute-start | bytes 589832 | tf_op jit(solution)/shard_map/ppermute | solution.py:28
  54.9 11.1 %collective-permute-start.34 = (bf16[12,32,256]{2,1,0:T(8,128)(2,1)S(1)}, bf16[12,32,256]{2,1,0:T(8,128)(2,1)S(1)}, u32[]{:S(2)}, u32[]{:S(2)}) collective-permute-start(bf16[12,32,256]{2,1,0:T(8,128)(2,1)S(1)} %get-tuple-element.70), channel_id=1, source_target_pairs={{0,4},{1,5},{2,6},{3,7},{4,0},{5,1},{6,2},{7,3},{8,12},{9,13},{10,... | collective-permute-start | bytes 589832 | tf_op jit(solution)/shard_map/ppermute | solution.py:28
  55.5 10.4 %collective-permute-start.35 = (bf16[12,32,256]{2,1,0:T(8,128)(2,1)S(1)}, bf16[12,32,256]{2,1,0:T(8,128)(2,1)S(1)}, u32[]{:S(2)}, u32[]{:S(2)}) collective-permute-start(bf16[12,32,256]{2,1,0:T(8,128)(2,1)S(1)} %get-tuple-element.71), channel_id=1, source_target_pairs={{0,6},{1,7},{2,4},{3,5},{4,2},{5,3},{6,0},{7,1},{8,14},{9,15},{10,... | collective-permute-start | bytes 589832 | tf_op jit(solution)/shard_map/ppermute | solution.py:28
  67.1 7.5 %collective-permute-start.36 = (bf16[5,32,256]{2,1,0:T(8,128)(2,1)S(1)}, bf16[5,32,256]{2,1,0:T(8,128)(2,1)S(1)}, u32[]{:S(2)}, u32[]{:S(2)}) collective-permute-start(bf16[5,32,256]{2,1,0:T(8,128)(2,1)S(1)} %get-tuple-element.72.after_ref.refs_10_), channel_id=1, source_target_pairs={{0,8},{1,9},{2,10},{3,11},{4,12},{5,13},{6,14},{7,15},{8,16},{9,17... | collective-permute-start | bytes 245768 | tf_op jit(solution)/shard_map/ppermute | solution.py:28
  67.2 9.0 %collective-permute-start.37 = (bf16[5,32,256]{2,1,0:T(8,128)(2,1)S(1)}, bf16[5,32,256]{2,1,0:T(8,128)(2,1)S(1)}, u32[]{:S(2)}, u32[]{:S(2)}) collective-permute-start(bf16[5,32,256]{2,1,0:T(8,128)(2,1)S(1)} %get-tuple-element.76), channel_id=1, source_target_pairs={{0,10},{1,11},{2,8},{3,9},{4,14},{5,15},{6,12},{7,13},{8,18},{9,19... | collective-permute-start | bytes 245768 | tf_op jit(solution)/shard_map/ppermute | solution.py:28
  67.6 10.1 %collective-permute-start.38 = (bf16[5,32,256]{2,1,0:T(8,128)(2,1)S(1)}, bf16[5,32,256]{2,1,0:T(8,128)(2,1)S(1)}, u32[]{:S(2)}, u32[]{:S(2)}) collective-permute-start(bf16[5,32,256]{2,1,0:T(8,128)(2,1)S(1)} %get-tuple-element.77), channel_id=1, source_target_pairs={{0,12},{1,13},{2,14},{3,15},{4,8},{5,9},{6,10},{7,11},{8,20},{9,21... | collective-permute-start | bytes 245768 | tf_op jit(solution)/shard_map/ppermute | solution.py:28
  69.3 9.7 %collective-permute-start.39 = (bf16[5,32,256]{2,1,0:T(8,128)(2,1)S(1)}, bf16[5,32,256]{2,1,0:T(8,128)(2,1)S(1)}, u32[]{:S(2)}, u32[]{:S(2)}) collective-permute-start(bf16[5,32,256]{2,1,0:T(8,128)(2,1)S(1)} %get-tuple-element.78), channel_id=1, source_target_pairs={{0,14},{1,15},{2,12},{3,13},{4,10},{5,11},{6,8},{7,9},{8,22},{9,23... | collective-permute-start | bytes 245768 | tf_op jit(solution)/shard_map/ppermute | solution.py:28
  84.0 8.0 %collective-permute-start.51 = (bf16[12,32,256]{2,1,0:T(8,128)(2,1)S(1)}, bf16[12,32,256]{2,1,0:T(8,128)(2,1)S(1)}, u32[]{:S(2)}, u32[]{:S(2)}) collective-permute-start(bf16[12,32,256]{2,1,0:T(8,128)(2,1)S(1)} %get-tuple-element.80), channel_id=1, source_target_pairs={{0,2},{1,3},{2,0},{3,1},{4,6},{5,7},{6,4},{7,5},{8,10},{9,11},{10,... | collective-permute-start | bytes 589832 | tf_op jit(solution)/shard_map/ppermute | solution.py:28
  85.4 11.1 %collective-permute-start.52 = (bf16[12,32,256]{2,1,0:T(8,128)(2,1)S(1)}, bf16[12,32,256]{2,1,0:T(8,128)(2,1)S(1)}, u32[]{:S(2)}, u32[]{:S(2)}) collective-permute-start(bf16[12,32,256]{2,1,0:T(8,128)(2,1)S(1)} %get-tuple-element.82), channel_id=1, source_target_pairs={{0,4},{1,5},{2,6},{3,7},{4,0},{5,1},{6,2},{7,3},{8,12},{9,13},{10,... | collective-permute-start | bytes 589832 | tf_op jit(solution)/shard_map/ppermute | solution.py:28
  86.1 10.4 %collective-permute-start.53 = (bf16[12,32,256]{2,1,0:T(8,128)(2,1)S(1)}, bf16[12,32,256]{2,1,0:T(8,128)(2,1)S(1)}, u32[]{:S(2)}, u32[]{:S(2)}) collective-permute-start(bf16[12,32,256]{2,1,0:T(8,128)(2,1)S(1)} %get-tuple-element.83), channel_id=1, source_target_pairs={{0,6},{1,7},{2,4},{3,5},{4,2},{5,3},{6,0},{7,1},{8,14},{9,15},{10,... | collective-permute-start | bytes 589832 | tf_op jit(solution)/shard_map/ppermute | solution.py:28
  (31 other events, 93.0 us)
